TPU v7x, 32 devices: a whole 2x2x4 slice. The times are simulated.
32 devices in a mesh: ctx: 8 (over y, x, core), fsdp: 4 (over z).
Axes of the slice: x: 2, y: 2, z: 4, core: 2. Of those that a mesh axis runs over, the one named last changes fastest.
Arguments:
- tokens_in: bfloat16 [4, 1024, 1024], P('fsdp', 'ctx'), may hold values from -6 to 6
- doc_lengths: int32 [4, 8], P('fsdp'), may hold values from 1 to 512, 1024 in all within a row
- norm1_gain: bfloat16 [1024], P('fsdp'), may hold values from 0.5 to 1.5
- norm1_bias: bfloat16 [1024], P('fsdp'), may hold values from -1.5 to 1.5
- qkv_weight: bfloat16 [1024, 3072], P('fsdp'), may hold values from -0.1875 to 0.1875
- qv_bias: bfloat16 [2048], P('fsdp'), may hold values from -1.5 to 1.5
- out_weight: bfloat16 [1024, 1024], P('fsdp'), may hold values from -1.5 to 1.5
- out_bias: bfloat16 [1024], P('fsdp'), may hold values from -1.5 to 1.5
- norm2_gain: bfloat16 [1024], P('fsdp'), may hold values from 0.5 to 1.5
- norm2_bias: bfloat16 [1024], P('fsdp'), may hold values from -1.5 to 1.5
- up_weight: bfloat16 [1024, 4096], P('fsdp'), may hold values from -0.1875 to 0.1875
- up_bias: bfloat16 [4096], P('fsdp'), may hold values from -1.5 to 1.5
- down_weight: bfloat16 [4096, 1024], P('fsdp'), may hold values from -0.09375 to 0.09375
- down_bias: bfloat16 [1024], P('fsdp'), may hold values from -1.5 to 1.5
- out_cotangent: bfloat16 [4, 1024, 1024], P('fsdp', 'ctx'), may hold values from -6 to 6
Outputs:
- layer_out: bfloat16 [4, 1024, 1024], P('fsdp', 'ctx')
- input_grad: bfloat16 [4, 1024, 1024], P('fsdp', 'ctx')
- norm1_gain_grad: float32 [1024], P(('ctx', 'fsdp'))
- norm1_bias_grad: float32 [1024], P(('ctx', 'fsdp'))
- qkv_weight_grad: float32 [1024, 3072], P(('ctx', 'fsdp'))
- qv_bias_grad: float32 [2048], P(('ctx', 'fsdp'))
- out_weight_grad: float32 [1024, 1024], P(('ctx', 'fsdp'))
- out_bias_grad: float32 [1024], P(('ctx', 'fsdp'))
- norm2_gain_grad: float32 [1024], P(('ctx', 'fsdp'))
- norm2_bias_grad: float32 [1024], P(('ctx', 'fsdp'))
- up_weight_grad: float32 [1024, 4096], P(('ctx', 'fsdp'))
- up_bias_grad: float32 [4096], P(('ctx', 'fsdp'))
- down_weight_grad: float32 [4096, 1024], P(('ctx', 'fsdp'))
- down_bias_grad: float32 [1024], P(('ctx', 'fsdp'))
Inputs may be any that keep to these rules, and one draw needn't show every extreme that they name: `doc_lengths`: each row lists one stream's documents in order; they sum to 1024; the longest is 512.
All inputs are finite; a program needn't handle non-finite values.
Results may differ from a plain program's by a relative error of at most 0.018.
Values may be sent and summed in bfloat16 or wider, within the bound.
A program may use at most 128 MiB of HBM per device.

v0:
```python
import functools
import jax
import jax.numpy as jnp
from jax import lax
from jax.experimental import pallas as pl
from jax.experimental.pallas import tpu as pltpu
from jax.sharding import PartitionSpec as P

HEADS = 16
HEAD_DIM = 64
MESH = pl.DeviceIdType.MESH

epsilon = 1e-05
masked_score = -1e30
score_scale = HEAD_DIM ** (-0.5)
f32 = jnp.float32
bf16 = jnp.bfloat16


def row_stats(values):
    mean = jnp.mean(values, axis=-1, keepdims=True)
    centre = values - mean
    spread = jnp.mean(centre * centre, axis=-1, keepdims=True)
    scale = lax.rsqrt(spread + epsilon)
    return centre * scale, scale


def norm_back(grad, xhat, scale, gain):
    gh = grad * gain
    return scale * (
        gh
        - jnp.mean(gh, axis=-1, keepdims=True)
        - xhat * jnp.mean(gh * xhat, axis=-1, keepdims=True)
    )


def gelu_both(v):
    k = 0.7978845608028654
    square = v * v
    inner = jnp.tanh(k * v * (1.0 + 0.044715 * square))
    half = 0.5 * (1.0 + inner)
    slope = half + 0.5 * v * (1.0 - inner * inner) * (k * (1.0 + 3 * 0.044715 * square))
    return v * half, slope


def mm(a, b, dims):
    return lax.dot_general(a, b, (dims, ((), ())), preferred_element_type=f32)


NN = ((1,), (0,))
NT = ((1,), (1,))
TN = ((0,), (0,))


def column_sum(v):
    return jnp.sum(v, axis=0, keepdims=True)


def bits(n):
    out = []
    while n > 1:
        n //= 2
        out.append(n)
    return out


class Net:
    def __init__(self, chips, Z, sems):
        self.chips, self.Z, self.C = chips, Z, 2 * chips
        self.c = lax.axis_index("ctx")
        self.z = lax.axis_index("fsdp")
        self.sems, self.used = sems, 0
        block = self.z * self.C + self.c
        self.home = (block // Z, block % Z)
        mine = self.c * Z + self.z
        self.origin = (mine % self.C, mine // self.C)
        self.at_home = block == mine

    def take(self, count):
        self.used += count
        return self.used - count

    def barrier(self):
        sem = pltpu.get_barrier_semaphore()
        peers = [(self.c ^ d, self.z) for d in range(1, self.C)]
        peers += [(self.c, self.z ^ d) for d in range(1, self.Z)]
        for peer in peers:
            pl.semaphore_signal(sem, inc=1, device_id=peer, device_id_type=MESH)

        @pl.when(jnp.logical_not(self.at_home))
        def _():
            for peer in (self.home, self.origin):
                pl.semaphore_signal(sem, inc=1, device_id=peer, device_id_type=MESH)

        pl.semaphore_wait(sem, len(peers) + jnp.where(self.at_home, 0, 2))

    def to(self, device, src, dst, out, into):
        return pltpu.make_async_remote_copy(
            src, dst, self.sems.at[0, out], self.sems.at[1, into],
            device_id=device, device_id_type=MESH,
        )

    def to_ctx(self, d, src, dst, i):
        return self.to((self.c ^ d, self.z), src, dst, i, i)

    def to_z(self, d, src, dst, i):
        return self.to((self.c, self.z ^ d), src, dst, i, i)


class ZGather:
    def __init__(self, net, dst):
        self.net, self.dst = net, dst
        self.base = net.take(net.Z)
        self.copies, self.got = {}, {0}

    def send(self, e, d):
        part = self.dst.at[self.net.z ^ e]
        copy = self.net.to_z(d, part, part, self.base + (e ^ d))
        copy.start()
        self.copies[e ^ d] = copy

    def begin(self):
        for d in bits(self.net.Z):
            self.send(0, d)

    def receive(self, e):
        if e not in self.got:
            self.copies[e].wait_recv()
            self.got.add(e)

    def relay(self):
        held = [0]
        for d in bits(self.net.Z):
            for e in held[1:]:
                self.receive(e)
                self.send(e, d)
            held = held + [e ^ d for e in held]

    def wait(self):
        for e in range(self.net.Z):
            self.receive(e)

    def finish(self):
        for copy in self.copies.values():
            copy.wait_send()


class ZReduce:
    def __init__(self, net, shard, recv, sums):
        self.net, self.shard, self.recv, self.sums = net, shard, recv, sums
        self.base = net.take(net.Z)
        self.terms = {e: [shard(net.z ^ e)] for e in range(net.Z)}
        self.copies, self.slot, self.full = [], 0, 0
        self.stages = bits(net.Z)[::-1]
        self.pending = {}

    def load(self, e):
        if e in self.pending:
            for copy in self.pending.pop(e):
                copy.wait_recv()
        total = None
        for ref in self.terms[e]:
            v = ref[...].astype(f32)
            total = v if total is None else total + v
        return total

    def stage(self, d):
        go = [e for e in sorted(self.terms) if e & d]
        for e in go:
            ref = self.terms[e][0]
            if len(self.terms[e]) > 1:
                total = self.load(e)
                ref = self.sums.at[self.full]
                self.full += 1
                ref[...] = total.astype(bf16)
            del self.terms[e]
            keep = e ^ d
            into = self.recv.at[self.slot]
            copy = self.net.to_z(d, ref, into, self.base + self.slot)
            copy.start()
            self.slot += 1
            self.copies.append(copy)
            self.pending.setdefault(keep, []).append(copy)
            self.terms[keep].append(into)

    def begin(self):
        self.stage(self.stages[0])

    def relay(self):
        for d in self.stages[1:]:
            self.stage(d)

    def total(self):
        return self.load(0)

    def finish(self):
        for copy in self.copies:
            copy.wait_send()


class Gather:
    def __init__(self, net, src, dst):
        self.net, self.src, self.dst = net, src, dst
        self.base = net.take(13 if net.chips == 4 else net.C)
        self.sent = []

    def copy(self, d, src, dst, i):
        copy = self.net.to_ctx(d, src, dst, self.base + i)
        copy.start()
        self.sent.append(copy)
        return copy

    def block(self, d, rows=None):
        index = self.net.c ^ d
        return self.dst.at[index] if rows is None else self.dst.at[index, rows]

    def begin(self):
        c = self.net.c
        if self.net.chips == 4:
            half = self.src.shape[0] // 2
            self.lo, self.hi = pl.ds(0, half), pl.ds(half, half)
            lo, hi, src, own = self.lo, self.hi, self.src, self.dst.at[c]
            self.x_lo = self.copy(2, src.at[lo], self.dst.at[c, lo], 0)
            self.y_hi = self.copy(4, src.at[hi], self.dst.at[c, hi], 1)
            self.x_hi = self.copy(2, src.at[hi], self.dst.at[c, hi], 2)
            self.y_lo = self.copy(4, src.at[lo], self.dst.at[c, lo], 3)
            self.beside = self.copy(1, src, own, 4)
        else:
            self.far = {
                d: self.copy(2 * d, self.src, self.dst.at[c], 2 * d)
                for d in range(self.net.chips - 1, 0, -1)
            }
            self.beside = self.copy(1, self.src, self.dst.at[c], 1)

    def relay(self, d, rows, target, i):
        part = self.block(d, rows)
        return self.copy(target, part, part, i)

    def middle(self):
        if self.net.chips == 4:
            self.x_lo.wait_recv()
            self.r_lo = self.relay(2, self.lo, 4, 5)
            self.s0 = self.relay(2, self.lo, 1, 6)
            self.y_hi.wait_recv()
            self.r_hi = self.relay(4, self.hi, 2, 7)
            self.s1 = self.relay(4, self.hi, 1, 8)

    def finish(self, ready=None):
        ready = ready or (lambda d: None)
        self.beside.wait_recv()
        ready(1)
        if self.net.chips == 4:
            self.x_hi.wait_recv()
            s2 = self.relay(2, self.hi, 1, 9)
            ready(2)
            self.y_lo.wait_recv()
            s3 = self.relay(4, self.lo, 1, 10)
            ready(4)
            self.r_lo.wait_recv()
            s4 = self.relay(6, self.lo, 1, 11)
            self.r_hi.wait_recv()
            s5 = self.relay(6, self.hi, 1, 12)
            ready(6)
            self.s0.wait_recv()
            s2.wait_recv()
            ready(3)
            self.s1.wait_recv()
            s3.wait_recv()
            ready(5)
            s4.wait_recv()
            s5.wait_recv()
            ready(7)
        else:
            on = {}
            for d, copy in self.far.items():
                copy.wait_recv()
                on[d] = self.relay(2 * d, None, 1, 2 * d + 1)
                ready(2 * d)
            for d, copy in on.items():
                copy.wait_recv()
                ready(2 * d + 1)
        for copy in self.sent:
            copy.wait_send()


class Reduce:
    def __init__(self, net, sib_send, sib_recv, far_send, far_recv, keep):
        self.net = net
        self.base = net.take(2 * net.chips)
        self.sib_send, self.sib_recv = sib_send, sib_recv
        self.far_send, self.far_recv, self.keep = far_send, far_recv, keep
        self.sib, self.far = {}, {}

    def pass_on(self, d):
        self.sib[d].wait_recv()
        total = self.keep[d] + self.sib_recv[d].astype(f32)
        self.far_send[d] = total.astype(bf16)
        self.far[d] = self.net.to_ctx(
            2 * d, self.far_send.at[d], self.far_recv.at[d], self.base + self.net.chips + d
        )
        self.far[d].start()

    def begin(self, partial):
        net = self.net
        core, chip = net.c % 2, net.c // 2
        last = None
        for d in range(net.chips - 1, -1, -1):
            terms = partial(chip ^ d)
            rows = terms.shape[0] // 2
            low, high = terms[:rows], terms[rows:]
            self.sib_send[d] = jnp.where(core == 0, high, low).astype(bf16)
            self.sib[d] = net.to_ctx(1, self.sib_send.at[d], self.sib_recv.at[d], self.base + d)
            self.sib[d].start()
            self.keep[d] = jnp.where(core == 0, low, high)
            if last is not None:
                self.pass_on(last)
            last = d

    def finish(self):
        self.sib[0].wait_recv()
        total = self.keep[0] + self.sib_recv[0].astype(f32)
        for d in range(self.net.chips - 1, 0, -1):
            self.far[d].wait_recv()
            total = total + self.far_recv[d].astype(f32)
        for copy in list(self.sib.values()) + list(self.far.values()):
            copy.wait_send()
        return total


class Swap:
    def __init__(self, net, parts, dst):
        self.net, self.parts, self.dst = net, parts, dst
        self.base = net.take(net.C)

    def start(self):
        net = self.net
        self.copies = [
            net.to_ctx(d, self.parts.at[net.c ^ d], self.dst.at[net.c], self.base + d)
            for d in range(net.C - 1, 0, -1)
        ]
        for copy in self.copies:
            copy.start()
        self.dst[net.c] = self.parts[net.c]

    def wait(self):
        for copy in self.copies:
            copy.wait()


class Spread:
    def __init__(self, net, dst, plane):
        self.net, self.dst, self.plane = net, dst, plane
        self.base = net.take(net.C if plane else net.Z)

    def start(self):
        net = self.net
        part = self.dst.at[net.c if self.plane else net.z]
        send = net.to_ctx if self.plane else net.to_z
        count = net.C if self.plane else net.Z
        self.copies = [send(d, part, part, self.base + d) for d in range(count - 1, 0, -1)]
        for copy in self.copies:
            copy.start()

    def wait(self):
        for copy in self.copies:
            copy.wait()


class Route:
    def __init__(self, net, parts, dst, local):
        self.net, self.parts, self.dst, self.local = net, parts, dst, local
        self.base = net.take(net.Z)
        self.per = net.C // net.Z

    def each(self, remote, own):
        net = self.net
        slot = net.c % net.Z
        for z in range(net.Z):
            target = z * self.per + net.c // net.Z
            copy = net.to(
                (target, net.z), self.parts.at[z], self.dst.at[slot], self.base + z, self.base + slot
            )
            here = pltpu.make_async_copy(self.parts.at[z], self.dst.at[slot], self.local)

            @pl.when(target != net.c)
            def _():
                remote(copy)

            @pl.when(target == net.c)
            def _():
                own(here)

    def start(self):
        self.each(lambda copy: copy.start(), lambda here: here.start())

    def wait(self):
        net = self.net
        for s in range(net.Z):
            source = (net.c % self.per) * net.Z + s

            @pl.when(source != net.c)
            def _():
                part = self.dst.at[s]
                net.to((net.c ^ 1, net.z), part, part, self.base + s, self.base + s).wait_recv()

        self.each(lambda copy: copy.wait_send(), lambda here: here.wait())


class Vectors:
    names = ("gain1", "shift1", "qv", "out", "gain2", "shift2", "up", "down")

    def __init__(self, ref, Z, sizes):
        self.ref, self.Z, self.at = ref, Z, {}
        start = 0
        for name, size in zip(self.names, sizes):
            self.at[name] = (start, size)
            start += size

    def get(self, name):
        start, size = self.at[name]
        return jnp.concatenate(
            [self.ref[z, :, start : start + size] for z in range(self.Z)], axis=1
        )


def chosen(pieces, index):
    out = jnp.zeros_like(pieces[0])
    for i, piece in enumerate(pieces):
        out = jnp.where(index == i, piece, out)
    return out


def layer_kernel(names, chips, Z, sizes, aligned, *refs):
    ref = dict(zip(names, refs))
    net = Net(chips, Z, ref["sems"])
    local = ref["local"]
    c, z, C = net.c, net.z, net.C
    x_in, cot_in = ref["x_in"], ref["cot_in"]
    R, D = x_in.shape
    S = R * C
    hw = ref["mix"].shape[1]
    heads = hw // HEAD_DIM
    fw = ref["hid"].shape[1]
    fzc = fw // Z
    r = D // (C * Z)
    step = 2 * R
    xs, n1, n2, cot, bg = (ref[k] for k in ("xs", "n1", "n2", "cot", "bg"))
    qkv, mix, lse = ref["qkv"], ref["mix"], ref["lse"]

    started = []

    def bring(src, dst, i):
        copy = pltpu.make_async_copy(src, dst, local.at[i])
        copy.start()
        return copy

    load_vec = [bring(ref["vec_in"], ref["vec"].at[z], 0)]
    load_x = bring(x_in, xs.at[c], 1)
    if aligned:
        load_q = [
            bring(
                ref["wqkv_in"].at[:, pl.ds(pl.multiple_of(p * D + c * hw, hw), hw)],
                ref["wqkv"].at[z, :, p * hw : (p + 1) * hw], 2 + p,
            )
            for p in range(3)
        ]
        FZ = fzc * C
        load_u = [
            bring(
                ref["wup_in"].at[:, pl.ds(pl.multiple_of(p * FZ + c * fzc, fzc), fzc)],
                ref["wup"].at[z, :, p * fzc : (p + 1) * fzc], 8 + p,
            )
            for p in range(Z)
        ]
    else:
        load_q = [bring(ref["wqkv_in"], ref["wqkv"].at[z], 2)]
        load_u = [bring(ref["wup_in"], ref["wup"].at[z], 8)]
    load_o = bring(ref["wout_in"].at[pl.ds(pl.multiple_of(c * r, r), r)], ref["wout_parts"].at[z], 5)
    load_d = bring(ref["wdown_in"].at[pl.ds(pl.multiple_of(c * fzc, fzc), fzc)], ref["wdown"].at[z], 6)
    load_c = bring(cot_in, cot.at[c], 7)

    zv, zq = ZGather(net, ref["vec"]), ZGather(net, ref["wqkv"])
    zo, zu = ZGather(net, ref["wout_parts"]), ZGather(net, ref["wup"])
    zd = ZGather(net, ref["wdown"])
    net.barrier()
    load_vec[0].wait()
    zv.begin()
    gx = Gather(net, x_in, xs)
    gx.begin()
    for copy in load_q:
        copy.wait()
    zq.begin()

    pos = lax.broadcasted_iota(jnp.int32, (S, 1), 0)
    first = jnp.zeros((S, 1), jnp.int32)
    end = jnp.int32(0)
    for i in range(ref["docs"].shape[1]):
        end = end + ref["docs"][0, i]
        first = jnp.where(pos >= end, end, first)
    ref["first"][...] = first

    zv.relay()
    zv.wait()
    vectors = Vectors(ref["vec"], Z, sizes)
    gain1, shift1 = vectors.get("gain1"), vectors.get("shift1")
    load_x.wait()

    def norm_one(d):
        block = c ^ d
        xhat, _ = row_stats(xs[block].astype(f32))
        n1[block] = (xhat * gain1 + shift1).astype(bf16)

    norm_one(0)
    gx.middle()
    zq.relay()
    gx.finish(norm_one)
    load_o.wait()
    zo.begin()
    for copy in load_u:
        copy.wait()
    zu.begin()
    load_c.wait()
    gc = Gather(net, cot_in, cot)
    gc.begin()

    qv = vectors.get("qv")
    bias = jnp.concatenate(
        [
            chosen([qv[:, i * hw : (i + 1) * hw] for i in range(C)], c),
            jnp.zeros((1, hw), f32),
            chosen([qv[:, D + i * hw : D + (i + 1) * hw] for i in range(C)], c),
        ],
        axis=1,
    )
    zq.wait()
    w_qkv = ref["wqkv"][...].reshape(D, 3 * hw)

    def blocks(array, i):
        return array[pl.ds(2 * i, 2)].reshape(step, D)

    def tile(i):
        return pl.ds(pl.multiple_of(i * step, step), step)

    def project(i, carry):
        qkv[tile(i), :] = (mm(blocks(n1, i), w_qkv, NN) + bias).astype(bf16)
        return carry

    lax.fori_loop(0, S // step, project, 0)
    gc.middle()
    zo.relay()

    route = Route(net, ref["wout_parts"], ref["wout"], local.at[5])
    tiles = S // step

    def masked(i):
        n = (i + 1) * step
        row = lax.broadcasted_iota(jnp.int32, (step, n), 0) + i * step
        col = lax.broadcasted_iota(jnp.int32, (step, n), 1)
        return (col <= row) & (col >= ref["first"][i * step : n, :])

    def head(part, h, rows):
        at = part * hw + h * HEAD_DIM
        return qkv[rows, at : at + HEAD_DIM]

    def beside(parts):
        return jnp.concatenate(parts, axis=1) if len(parts) > 1 else parts[0]

    for i in range(tiles):
        if i == tiles - 2:
            zo.wait()
            route.start()
            zu.relay()
            load_d.wait()
            zd.begin()
        n = (i + 1) * step
        rows, keys = slice(i * step, n), slice(0, n)
        allowed = masked(i)
        parts = []
        for h in range(heads):
            s = mm(head(0, h, rows), head(1, h, keys), NT) * score_scale
            s = jnp.where(allowed, s, masked_score)
            top = jnp.max(s, axis=1, keepdims=True)
            e = jnp.exp(s - top)
            total = jnp.sum(e, axis=1, keepdims=True)
            parts.append((mm(e.astype(bf16), head(2, h, keys), NN) / total).astype(bf16))
            lse[h, rows, :] = top + jnp.log(total)
        mix[rows, :] = beside(parts)
    gc.finish()
    route.wait()
    w_out = ref["wout"][...].reshape(hw, D)

    def reducer(k):
        return Reduce(
            net, ref["sib_send"], ref["sib_recv"].at[k % 2], ref["far_send"], ref["far_recv"].at[k % 2],
            ref["keep"],
        )

    red = reducer(0)
    red.begin(lambda chip: mm(mix[tile(chip), :], w_out, NN))
    zd.relay()
    total = red.finish()
    resid = xs[c].astype(f32) + total + vectors.get("out")
    xhat2, scale2 = row_stats(resid)
    gain2 = vectors.get("gain2")
    n2[c] = (xhat2 * gain2 + vectors.get("shift2")).astype(bf16)
    ref["resid"][...] = resid
    gn = Gather(net, n2.at[c], n2)
    gn.begin()
    gn.middle()
    zu.wait()
    w_up = ref["wup"][...].reshape(D, fw)
    up = vectors.get("up")
    b_up = jnp.concatenate(
        [
            chosen([up[:, (q * C + i) * fzc : (q * C + i + 1) * fzc] for i in range(C)], c)
            for q in range(Z)
        ],
        axis=1,
    )
    gn.finish()
    zd.wait()
    w_down = ref["wdown"][...].reshape(fw, D)
    hid, pg = ref["hid"], ref["pg"]

    def feed(i, sums):
        rows = tile(i)
        value, slope = gelu_both(mm(blocks(n2, i), w_up, NN) + b_up)
        hid[rows, :] = value.astype(bf16)
        grad = (mm(blocks(cot, i), w_down, NT) * slope).astype(bf16)
        pg[rows, :] = grad
        return sums + column_sum(grad.astype(f32))

    up_sums = lax.fori_loop(0, tiles, feed, jnp.zeros((1, fw), f32))

    red = reducer(1)
    red.begin(lambda chip: mm(pg[tile(chip), :], w_up, NT))

    lanes = 128

    def whole(array):
        return array[...].reshape(S, D)

    def chunk(i):
        return pl.ds(pl.multiple_of(i * lanes, lanes), lanes)

    dbuf, ubuf, obuf, qbuf = (ref[k] for k in ("dbuf", "ubuf", "obuf", "qbuf"))

    def down_part(i, carry):
        dbuf[chunk(i), :] = mm(hid[:, chunk(i)], whole(cot), TN).astype(bf16)
        return carry

    lax.fori_loop(0, fw // lanes, down_part, 0)
    rd = ZReduce(
        net, lambda zs: dbuf.at[pl.ds(pl.multiple_of(zs * fzc, fzc), fzc)], ref["drecv"], ref["dsum"]
    )
    rd.begin()
    per = lanes // (Z * r)

    def up_part(i, carry):
        grad = mm(n2[:, :, chunk(i)].reshape(S, lanes), pg[...], TN).astype(bf16)
        ubuf[pl.ds(i * per, per)] = grad.reshape(per, Z, r, fw)
        return carry

    lax.fori_loop(0, D // lanes, up_part, 0)
    ru = ZReduce(net, lambda zs: ubuf.at[:, zs], ref["urecv"], ref["usum"])
    ru.begin()

    n2_grad = red.finish()
    cot_own = cot[c].astype(f32)
    xhat2, scale2 = row_stats(ref["resid"][...])
    resid_grad = cot_own + norm_back(n2_grad, xhat2, scale2, gain2)
    branch = resid_grad.astype(bf16)
    bg[c] = branch
    ref["rgrad"][...] = resid_grad
    gb = Gather(net, bg.at[c], bg)
    gb.begin()
    sums = {
        "out": column_sum(branch.astype(f32)),
        "gain2": column_sum(n2_grad * xhat2),
        "shift2": column_sum(n2_grad),
        "down": column_sum(cot_own),
    }
    mg = ref["mg"]

    def back_out(d):
        block = c ^ d
        rows = pl.ds(pl.multiple_of(block * R, R), R)
        mg[rows, :] = mm(bg[block], w_out, NT).astype(bf16)

    back_out(0)
    gb.middle()
    rd.relay()
    gb.finish(back_out)
    obuf[...] = mm(mix[...], whole(bg), TN).astype(bf16)
    ro = ZReduce(
        net, lambda zs: obuf.at[pl.ds(pl.multiple_of(zs * r, r), r)], ref["orecv"], ref["osum"]
    )
    ro.begin()
    red = reducer(2)
    red.begin(lambda chip: mm(hid[tile(chip), :], w_down, NN))

    qg, dk, dv = ref["qg"], ref["dk"], ref["dv"]
    dk[...] = jnp.zeros((S, hw), f32)
    dv[...] = jnp.zeros((S, hw), f32)
    swap_up = Swap(net, ref["uparts"], ref["ufrom"])
    for i in range(tiles):
        n = (i + 1) * step
        rows, keys = slice(i * step, n), slice(0, n)
        allowed = masked(i)
        dqs, dks, dvs = [], [], []
        for h in range(heads):
            at = h * HEAD_DIM
            q, k, v = head(0, h, rows), head(1, h, keys), head(2, h, keys)
            g = mg[rows, at : at + HEAD_DIM]
            m = mix[rows, at : at + HEAD_DIM]
            s = mm(q, k, NT) * score_scale - lse[h, rows, :]
            p = jnp.where(allowed, jnp.exp(s), 0.0)
            delta = jnp.sum(g.astype(f32) * m.astype(f32), axis=1, keepdims=True)
            ds = (p * (mm(g, v, NT) - delta)).astype(bf16)
            dqs.append(score_scale * mm(ds, k, NN))
            dks.append(mm(ds, q, TN))
            dvs.append(mm(p.astype(bf16), g, TN))
        qg[rows, 0:hw] = beside(dqs).astype(bf16)
        dk[keys, :] += beside(dks)
        dv[keys, :] += beside(dvs)
        if i == tiles - 3:
            ref["hbuf"][...] = rd.total().astype(bf16)
            there = net.to(net.home, ref["hbuf"], ref["hrecv"], net.take(1), net.used - 1)
            here = pltpu.make_async_copy(ref["hbuf"], ref["hrecv"], local.at[0])

            @pl.when(net.at_home)
            def _():
                here.start()

            @pl.when(jnp.logical_not(net.at_home))
            def _():
                there.start()

            ru.relay()
        if i == tiles - 2:
            total = red.finish()
            ref["layer_out"][...] = (ref["resid"][...] + total + vectors.get("down")).astype(bf16)
            ro.relay()
    qg[:, hw : 2 * hw] = (score_scale * dk[...]).astype(bf16)
    qg[:, 2 * hw : 3 * hw] = dv[...].astype(bf16)

    def qkv_part(i, carry):
        grad = mm(n1[:, :, chunk(i)].reshape(S, lanes), qg[...], TN).astype(bf16)
        qbuf[pl.ds(i * per, per)] = grad.reshape(per, Z, r, 3 * hw)
        return carry

    lax.fori_loop(0, D // lanes, qkv_part, 0)
    rq = ZReduce(net, lambda zs: qbuf.at[:, zs], ref["qrecv"], ref["qsum"])
    rq.begin()
    red = reducer(3)
    red.begin(lambda chip: mm(qg[tile(chip), :], w_qkv, NT))
    qkv_sums = column_sum(qg[...].astype(f32))
    ref["uparts"][...] = ru.total().astype(bf16)
    swap_up.start()
    ref["d_out"][...] = ro.total()
    colz, colp = ref["colz"], ref["colp"]
    colz[z] = jnp.concatenate([qkv_sums[:, 0:hw], qkv_sums[:, 2 * hw : 3 * hw], up_sums], axis=1)
    line = Spread(net, colz, False)
    line.start()

    @pl.when(net.at_home)
    def _():
        here.wait()

    @pl.when(jnp.logical_not(net.at_home))
    def _():
        there.wait()

    ref["d_down"][...] = ref["hrecv"][...].astype(f32)
    swap_up.wait()
    for i in range(C):
        for q in range(Z):
            ref["d_up"][:, (q * C + i) * fzc : (q * C + i + 1) * fzc] = ref["ufrom"][
                i, :, q * fzc : (q + 1) * fzc
            ].astype(f32)
    line.wait()
    total = colz[0]
    for i in range(1, Z):
        total = total + colz[i]
    colp[c] = total
    plane = Spread(net, colp, True)
    plane.start()
    rq.relay()
    n1_grad = red.finish()
    xhat1, scale1 = row_stats(xs[c].astype(f32))
    ref["input_grad"][...] = (
        ref["rgrad"][...] + norm_back(n1_grad, xhat1, scale1, gain1)
    ).astype(bf16)
    stack = jnp.concatenate(
        [
            column_sum(n1_grad * xhat1), column_sum(n1_grad), sums["out"], sums["gain2"],
            sums["shift2"], sums["down"], jnp.zeros((2, D), f32),
        ],
        axis=0,
    )
    w = D // C
    for i in range(C):
        ref["tok_to"][i] = stack[:, i * w : (i + 1) * w]
    swap_tok = Swap(net, ref["tok_to"], ref["tok_from"])
    swap_tok.start()
    ref["qparts"][...] = rq.total().astype(bf16)
    swap_q = Swap(net, ref["qparts"], ref["qfrom"])
    swap_q.start()
    swap_tok.wait()
    tokz = ref["tokz"]
    total = ref["tok_from"][0]
    for i in range(1, C):
        total = total + ref["tok_from"][i]
    tokz[z] = total
    tok_line = Spread(net, tokz, False)
    tok_line.start()
    swap_q.wait()
    for i in range(C):
        for p in range(3):
            ref["d_qkv"][:, p * D + i * hw : p * D + (i + 1) * hw] = ref["qfrom"][
                i, :, p * hw : (p + 1) * hw
            ].astype(f32)
    tok_line.wait()
    total = tokz[0]
    for i in range(1, Z):
        total = total + tokz[i]
    ref["tok"][...] = total
    plane.wait()
    for part in (zv, zq, zo, zu, zd, rd, ru, ro, rq):
        part.finish()


def shards(
    tokens_in,
    doc_lengths,
    norm1_gain,
    norm1_bias,
    qkv_weight,
    qv_bias,
    out_weight,
    out_bias,
    norm2_gain,
    norm2_bias,
    up_weight,
    up_bias,
    down_weight,
    down_bias,
    out_cotangent,
):
    C, Z = lax.axis_size("ctx"), lax.axis_size("fsdp")
    c, z = lax.axis_index("ctx"), lax.axis_index("fsdp")
    R, D = tokens_in.shape[1:]
    chips, S, hw = C // 2, R * C, D // C
    ff = up_weight.shape[1]
    fw, fzc, r = ff // C, ff // (C * Z), D // (C * Z)
    heads = hw // HEAD_DIM
    all_vectors = (
        norm1_gain, norm1_bias, qv_bias, out_bias, norm2_gain, norm2_bias, up_bias, down_bias
    )
    sizes = tuple(v.shape[0] for v in all_vectors)
    V, W = sum(sizes), 2 * hw + fw
    vec_in = jnp.concatenate(all_vectors).astype(f32)[None]
    aligned = hw % 128 == 0 and fzc % 128 == 0
    wqkv_in, wup_in = qkv_weight, up_weight
    if not aligned:
        wqkv_in = lax.dynamic_index_in_dim(
            qkv_weight.reshape(D // Z, 3, C, hw), c, axis=2, keepdims=False
        ).reshape(D // Z, 3 * hw)
        wup_in = lax.dynamic_index_in_dim(
            up_weight.reshape(D // Z, Z, C, fzc), c, axis=2, keepdims=False
        ).reshape(D // Z, fw)

    vmem, hbm = pltpu.VMEM, pl.BlockSpec(memory_space=pl.ANY)
    ins = {
        "x_in": (tokens_in[0], hbm),
        "cot_in": (out_cotangent[0], hbm),
        "docs": (doc_lengths, pl.BlockSpec(memory_space=pltpu.SMEM)),
        "vec_in": (vec_in, hbm),
        "wqkv_in": (wqkv_in, hbm),
        "wout_in": (out_weight, hbm),
        "wup_in": (wup_in, hbm),
        "wdown_in": (down_weight, hbm),
    }
    outs = {
        "layer_out": ((R, D), bf16),
        "input_grad": ((R, D), bf16),
        "d_qkv": ((r, 3 * D), f32),
        "d_out": ((r, D), f32),
        "d_up": ((r, ff), f32),
        "d_down": ((fzc, D), f32),
        "tok": ((8, D // C), f32),
        "colp": ((C, 1, W), f32),
    }
    token, own = (C, R, D), (R, D)
    exchange = {"far_send": bf16, "sib_send": bf16, "keep": f32}
    scratch = {
        **{k: (token, bf16) for k in ("xs", "n1", "n2", "cot", "bg")},
        "qkv": ((S, 3 * hw), bf16),
        "qg": ((S, 3 * hw), bf16),
        "mix": ((S, hw), bf16),
        "mg": ((S, hw), bf16),
        "lse": ((heads, S, 1), f32),
        "dk": ((S, hw), f32),
        "dv": ((S, hw), f32),
        "hid": ((S, fw), bf16),
        "pg": ((S, fw), bf16),
        "resid": (own, f32),
        "rgrad": (own, f32),
        "vec": ((Z, 1, V), f32),
        "wqkv": ((Z, D // Z, 3 * hw), bf16),
        "wout_parts": ((Z, r, D), bf16),
        "wout": ((Z, r, D), bf16),
        "wup": ((Z, D // Z, fw), bf16),
        "wdown": ((Z, fzc, D), bf16),
        "first": ((S, 1), jnp.int32),
        **{k: ((chips, R, D), t) for k, t in exchange.items()},
        "sib_recv": ((2, chips, R, D), bf16),
        "far_recv": ((2, chips, R, D), bf16),
        "dbuf": ((fw, D), bf16),
        "ubuf": ((C, Z, r, fw), bf16),
        "obuf": ((hw, D), bf16),
        "qbuf": ((C, Z, r, 3 * hw), bf16),
        "hbuf": ((fzc, D), bf16),
        "hrecv": ((fzc, D), bf16),
        "colz": ((Z, 1, W), f32),
        "tok_to": ((C, 8, D // C), f32),
        "tok_from": ((C, 8, D // C), f32),
        "tokz": ((Z, 8, D // C), f32),
    }
    shard = {"d": (fzc, D), "u": (C, r, fw), "o": (r, D), "q": (C, r, 3 * hw)}
    for k, shape in shard.items():
        scratch[k + "recv"] = ((Z - 1, *shape), bf16)
        scratch[k + "sum"] = ((Z // 2, *shape), bf16)
    for k in ("u", "q"):
        scratch[k + "parts"] = (shard[k], bf16)
        scratch[k + "from"] = (shard[k], bf16)
    gathers = 4 * max(13, C)
    count = gathers + 10 * Z + 8 * chips + 5 * C + 8
    names = (*ins, *outs, *scratch, "sems", "local")
    got = pl.pallas_call(
        functools.partial(layer_kernel, names, chips, Z, sizes, aligned),
        out_shape=[jax.ShapeDtypeStruct(*v) for v in outs.values()],
        in_specs=[v[1] for v in ins.values()],
        out_specs=[pl.BlockSpec(memory_space=vmem)] * len(outs),
        scratch_shapes=[vmem(*v) for v in scratch.values()]
        + [pltpu.SemaphoreType.DMA((2, count)), pltpu.SemaphoreType.DMA((8 + Z,))],
        compiler_params=pltpu.CompilerParams(
            collective_id=1, has_side_effects=True, vmem_limit_bytes=63 << 20
        ),
        name="layer",
    )(*[v[0] for v in ins.values()])
    got = dict(zip(outs, got))

    mine = c * Z + z
    tok = lax.dynamic_slice_in_dim(got["tok"], z * r, r, axis=1)
    col = got["colp"][:, 0]
    qv = jnp.concatenate([col[:, :hw].reshape(D), col[:, hw : 2 * hw].reshape(D)])
    up = col[:, 2 * hw :].reshape(C, Z, fzc).transpose(1, 0, 2).reshape(C * Z, fzc)
    return (
        got["layer_out"][None],
        got["input_grad"][None],
        tok[0],
        tok[1],
        got["d_qkv"],
        lax.dynamic_index_in_dim(qv.reshape(C * Z, -1), mine, keepdims=False),
        got["d_out"],
        tok[2],
        tok[3],
        tok[4],
        got["d_up"],
        lax.dynamic_index_in_dim(up, mine, keepdims=False),
        got["d_down"],
        tok[5],
    )


def solution(mesh):
    token = P("fsdp", "ctx", None)
    flat, table = P("fsdp"), P("fsdp", None)
    home, home2 = P(("ctx", "fsdp")), P(("ctx", "fsdp"), None)
    return jax.shard_map(
        shards,
        mesh=mesh,
        in_specs=(
            token, table, flat, flat, table, flat, table, flat,
            flat, flat, table, flat, table, flat, token,
        ),
        out_specs=(
            token, token, home, home, home2, home, home2, home,
            home, home, home2, home, home2, home,
        ),
        check_vma=False,
    )
```

profile of v0, /device:TPU:0, one launch (start us, length us, event | category | flops | bytes accessed | tf_op | source)
XLA Modules:
  0.0 186.0 jit_solution(13461017576420584068)
XLA Ops:
  0.7 0.7 constant_dynamic-update-slice_fusion.7
  1.3 0.7 constant_dynamic-update-slice_fusion.6
  2.0 0.7 constant_dynamic-update-slice_fusion.5
  2.7 0.7 constant_dynamic-update-slice_fusion.4
  3.3 0.7 constant_dynamic-update-slice_fusion.3
  4.0 0.7 constant_dynamic-update-slice_fusion.2
  4.7 0.7 constant_dynamic-update-slice_fusion.1
  5.3 0.7 constant_dynamic-update-slice_fusion
  6.0 0.6 convert_element_type.10.refs_3_
  6.6 168.7 %layer.1 = (bf16[128,1024]{1,0:T(8,128)(2,1)}, bf16[128,1024]{1,0:T(8,128)(2,1)}, f32[32,3072]{1,0:T(8,128)}, f32[32,1024]{1,0:T(8,128)}, f32[32,4096]{1,0:T(8,1...) custom-call(bf16[128,1024]{1,0:T(8,128)(2,1)} %bitcast.29, bf16[128,1024]{1,0:T(8,128)(2,1)} %bitcast.30, ...), custom_call_target="tpu_custom_call" | custom-call | tf_op jit(solution)/shard_map/layer/pallas_call | solution.py:940
  175.3 0.0 copy-start.2
  175.3 0.0 copy-start.1
  175.3 0.0 copy-start
  175.3 0.9 constant_dynamic-slice_fusion.1
  176.2 0.5 slice_bitcast_fusion.1
  176.7 0.7 copy.31
  177.5 0.5 fusion
  178.0 0.1 concatenate.43
  178.1 0.1 concatenate.44
  178.1 0.5 fusion.2
  178.6 1.7 copy.45
  180.3 1.7 copy.46
  182.0 1.8 copy.47
  183.7 0.0 copy-done.2
  183.8 0.7 copy.48
  184.4 0.0 copy-done.1
  184.4 0.8 copy.49
  185.2 0.0 copy-done
  185.2 0.8 copy.50
  (2 shorter events, 0.0 us)
Async XLA Ops:
  175.3 8.4 %copy-start.2 = (f32[32,1024]{1,0:T(8,128)S(1)}, f32[32,1024]{1,0:T(8,128)}, u32[]{:S(2)}) copy-start(f32[32,1024]{1,0:T(8,128)} %get-tuple-element.58) | copy-start | bytes 393220
  175.3 9.1 %copy-start.1 = (f32[32,4096]{1,0:T(8,128)S(1)}, f32[32,4096]{1,0:T(8,128)}, u32[]{:S(2)}) copy-start(f32[32,4096]{1,0:T(8,128)} %get-tuple-element.62) | copy-start | bytes 1572868
  175.3 9.9 %copy-start = (f32[128,1024]{1,0:T(8,128)S(1)}, f32[128,1024]{1,0:T(8,128)}, u32[]{:S(2)}) copy-start(f32[128,1024]{1,0:T(8,128)} %get-tuple-element.64) | copy-start | bytes 1572868
where the time goes:
time: 186 us
  Pallas kernels  169 us (91%)
  local copies, waits for them, and re-layouts  15.5 us (8%)
    pallas_call x1, Pallas kernels, shards(): pl.pallas_call(functools.partial(layer_kernel, names, chips, Z, sizes, al...  169 us
    unnamed x20, local copies, waits for them, and re-layouts  12.8 us

commit v1 on v0

--- a/solution.py
+++ b/solution.py
@@ -1,4 +1,6 @@
 import functools
+from types import SimpleNamespace
+
 import jax
 import jax.numpy as jnp
 from jax import lax
@@ -199,8 +201,8 @@
 
 
 class Gather:
-    def __init__(self, net, src, dst):
-        self.net, self.src, self.dst = net, src, dst
+    def __init__(self, net, src, place, rows):
+        self.net, self.src, self.place, self.rows = net, src, place, rows
         self.base = net.take(13 if net.chips == 4 else net.C)
         self.sent = []
 
@@ -210,31 +212,26 @@
         self.sent.append(copy)
         return copy
 
-    def block(self, d, rows=None):
-        index = self.net.c ^ d
-        return self.dst.at[index] if rows is None else self.dst.at[index, rows]
+    def own(self, d, rows, i):
+        return self.copy(d, self.src(rows), self.place(self.net.c, rows), i)
+
+    def relay(self, d, rows, target, i):
+        part = self.place(self.net.c ^ d, rows)
+        return self.copy(target, part, part, i)
 
     def begin(self):
-        c = self.net.c
+        every = pl.ds(0, self.rows)
         if self.net.chips == 4:
-            half = self.src.shape[0] // 2
+            half = self.rows // 2
             self.lo, self.hi = pl.ds(0, half), pl.ds(half, half)
-            lo, hi, src, own = self.lo, self.hi, self.src, self.dst.at[c]
-            self.x_lo = self.copy(2, src.at[lo], self.dst.at[c, lo], 0)
-            self.y_hi = self.copy(4, src.at[hi], self.dst.at[c, hi], 1)
-            self.x_hi = self.copy(2, src.at[hi], self.dst.at[c, hi], 2)
-            self.y_lo = self.copy(4, src.at[lo], self.dst.at[c, lo], 3)
-            self.beside = self.copy(1, src, own, 4)
+            self.x_lo = self.own(2, self.lo, 0)
+            self.y_hi = self.own(4, self.hi, 1)
+            self.x_hi = self.own(2, self.hi, 2)
+            self.y_lo = self.own(4, self.lo, 3)
+            self.beside = self.own(1, every, 4)
         else:
-            self.far = {
-                d: self.copy(2 * d, self.src, self.dst.at[c], 2 * d)
-                for d in range(self.net.chips - 1, 0, -1)
-            }
-            self.beside = self.copy(1, self.src, self.dst.at[c], 1)
-
-    def relay(self, d, rows, target, i):
-        part = self.block(d, rows)
-        return self.copy(target, part, part, i)
+            self.far = {d: self.own(2 * d, every, 2 * d) for d in range(self.net.chips - 1, 0, -1)}
+            self.beside = self.own(1, every, 1)
 
     def middle(self):
         if self.net.chips == 4:
@@ -271,10 +268,10 @@
             s5.wait_recv()
             ready(7)
         else:
-            on = {}
+            on, every = {}, pl.ds(0, self.rows)
             for d, copy in self.far.items():
                 copy.wait_recv()
-                on[d] = self.relay(2 * d, None, 1, 2 * d + 1)
+                on[d] = self.relay(2 * d, every, 1, 2 * d + 1)
                 ready(2 * d)
             for d, copy in on.items():
                 copy.wait_recv()
@@ -366,46 +363,6 @@
             copy.wait()
 
 
-class Route:
-    def __init__(self, net, parts, dst, local):
-        self.net, self.parts, self.dst, self.local = net, parts, dst, local
-        self.base = net.take(net.Z)
-        self.per = net.C // net.Z
-
-    def each(self, remote, own):
-        net = self.net
-        slot = net.c % net.Z
-        for z in range(net.Z):
-            target = z * self.per + net.c // net.Z
-            copy = net.to(
-                (target, net.z), self.parts.at[z], self.dst.at[slot], self.base + z, self.base + slot
-            )
-            here = pltpu.make_async_copy(self.parts.at[z], self.dst.at[slot], self.local)
-
-            @pl.when(target != net.c)
-            def _():
-                remote(copy)
-
-            @pl.when(target == net.c)
-            def _():
-                own(here)
-
-    def start(self):
-        self.each(lambda copy: copy.start(), lambda here: here.start())
-
-    def wait(self):
-        net = self.net
-        for s in range(net.Z):
-            source = (net.c % self.per) * net.Z + s
-
-            @pl.when(source != net.c)
-            def _():
-                part = self.dst.at[s]
-                net.to((net.c ^ 1, net.z), part, part, self.base + s, self.base + s).wait_recv()
-
-        self.each(lambda copy: copy.wait_send(), lambda here: here.wait())
-
-
 class Vectors:
     names = ("gain1", "shift1", "qv", "out", "gain2", "shift2", "up", "down")
 
@@ -431,21 +388,22 @@
 
 
 def layer_kernel(names, chips, Z, sizes, aligned, *refs):
-    ref = dict(zip(names, refs))
-    net = Net(chips, Z, ref["sems"])
-    local = ref["local"]
+    ref = SimpleNamespace(**dict(zip(names, refs)))
+    net = Net(chips, Z, ref.sems)
+    local = ref.local
     c, z, C = net.c, net.z, net.C
-    x_in, cot_in = ref["x_in"], ref["cot_in"]
+    x_in, cot_in = ref.x_in, ref.cot_in
     R, D = x_in.shape
     S = R * C
-    hw = ref["mix"].shape[1]
+    hw = ref.mix.shape[2]
     heads = hw // HEAD_DIM
-    fw = ref["hid"].shape[1]
+    fw = ref.hid.shape[1]
     fzc = fw // Z
     r = D // (C * Z)
     step = 2 * R
-    xs, n1, n2, cot, bg = (ref[k] for k in ("xs", "n1", "n2", "cot", "bg"))
-    qkv, mix, lse = ref["qkv"], ref["mix"], ref["lse"]
+    xs, n1, n2, cot = (ref.xs, ref.n1, ref.n2, ref.cot)
+    bg = xs
+    qkv, mix, lse = ref.qkv, ref.mix, ref.lse
 
     started = []
 
@@ -454,38 +412,42 @@
         copy.start()
         return copy
 
-    load_vec = [bring(ref["vec_in"], ref["vec"].at[z], 0)]
+    load_vec = [bring(ref.vec_in, ref.vec.at[z], 0)]
     load_x = bring(x_in, xs.at[c], 1)
     if aligned:
         load_q = [
             bring(
-                ref["wqkv_in"].at[:, pl.ds(pl.multiple_of(p * D + c * hw, hw), hw)],
-                ref["wqkv"].at[z, :, p * hw : (p + 1) * hw], 2 + p,
+                ref.wqkv_in.at[:, pl.ds(pl.multiple_of(p * D + c * hw, hw), hw)],
+                ref.wqkv.at[z, :, p * hw : (p + 1) * hw], 2 + p,
             )
             for p in range(3)
         ]
         FZ = fzc * C
         load_u = [
             bring(
-                ref["wup_in"].at[:, pl.ds(pl.multiple_of(p * FZ + c * fzc, fzc), fzc)],
-                ref["wup"].at[z, :, p * fzc : (p + 1) * fzc], 8 + p,
+                ref.wup_in.at[:, pl.ds(pl.multiple_of(p * FZ + c * fzc, fzc), fzc)],
+                ref.wup.at[z, :, p * fzc : (p + 1) * fzc], 8 + p,
             )
             for p in range(Z)
         ]
     else:
-        load_q = [bring(ref["wqkv_in"], ref["wqkv"].at[z], 2)]
-        load_u = [bring(ref["wup_in"], ref["wup"].at[z], 8)]
-    load_o = bring(ref["wout_in"].at[pl.ds(pl.multiple_of(c * r, r), r)], ref["wout_parts"].at[z], 5)
-    load_d = bring(ref["wdown_in"].at[pl.ds(pl.multiple_of(c * fzc, fzc), fzc)], ref["wdown"].at[z], 6)
+        load_q = [bring(ref.wqkv_in, ref.wqkv.at[z], 2)]
+        load_u = [bring(ref.wup_in, ref.wup.at[z], 8)]
+    load_o = bring(ref.wout_in.at[pl.ds(pl.multiple_of(c * r, r), r)], ref.wout_parts.at[z], 5)
+    load_d = bring(ref.wdown_in.at[pl.ds(pl.multiple_of(c * fzc, fzc), fzc)], ref.wdown.at[z], 6)
     load_c = bring(cot_in, cot.at[c], 7)
 
-    zv, zq = ZGather(net, ref["vec"]), ZGather(net, ref["wqkv"])
-    zo, zu = ZGather(net, ref["wout_parts"]), ZGather(net, ref["wup"])
-    zd = ZGather(net, ref["wdown"])
+    zv, zq = ZGather(net, ref.vec), ZGather(net, ref.wqkv)
+    zo, zu = ZGather(net, ref.wout_parts), ZGather(net, ref.wup)
+    zd = ZGather(net, ref.wdown)
     net.barrier()
     load_vec[0].wait()
     zv.begin()
-    gx = Gather(net, x_in, xs)
+
+    def tokens(src, dst):
+        return Gather(net, lambda rows: src.at[rows], lambda i, rows: dst.at[i, rows], R)
+
+    gx = tokens(x_in, xs)
     gx.begin()
     for copy in load_q:
         copy.wait()
@@ -494,14 +456,14 @@
     pos = lax.broadcasted_iota(jnp.int32, (S, 1), 0)
     first = jnp.zeros((S, 1), jnp.int32)
     end = jnp.int32(0)
-    for i in range(ref["docs"].shape[1]):
-        end = end + ref["docs"][0, i]
+    for i in range(ref.docs.shape[1]):
+        end = end + ref.docs[0, i]
         first = jnp.where(pos >= end, end, first)
-    ref["first"][...] = first
+    ref.first[...] = first
 
     zv.relay()
     zv.wait()
-    vectors = Vectors(ref["vec"], Z, sizes)
+    vectors = Vectors(ref.vec, Z, sizes)
     gain1, shift1 = vectors.get("gain1"), vectors.get("shift1")
     load_x.wait()
 
@@ -513,15 +475,15 @@
     norm_one(0)
     gx.middle()
     zq.relay()
-    gx.finish(norm_one)
     load_o.wait()
     zo.begin()
     for copy in load_u:
         copy.wait()
     zu.begin()
     load_c.wait()
-    gc = Gather(net, cot_in, cot)
+    gc = tokens(cot_in, cot)
     gc.begin()
+    gx.finish(norm_one)
 
     qv = vectors.get("qv")
     bias = jnp.concatenate(
@@ -532,8 +494,9 @@
         ],
         axis=1,
     )
+    gc.middle()
     zq.wait()
-    w_qkv = ref["wqkv"][...].reshape(D, 3 * hw)
+    w_qkv = ref.wqkv[...].reshape(D, 3 * hw)
 
     def blocks(array, i):
         return array[pl.ds(2 * i, 2)].reshape(step, D)
@@ -546,17 +509,15 @@
         return carry
 
     lax.fori_loop(0, S // step, project, 0)
-    gc.middle()
     zo.relay()
-
-    route = Route(net, ref["wout_parts"], ref["wout"], local.at[5])
+    gc.finish()
     tiles = S // step
 
     def masked(i):
         n = (i + 1) * step
         row = lax.broadcasted_iota(jnp.int32, (step, n), 0) + i * step
         col = lax.broadcasted_iota(jnp.int32, (step, n), 1)
-        return (col <= row) & (col >= ref["first"][i * step : n, :])
+        return (col <= row) & (col >= ref.first[i * step : n, :])
 
     def head(part, h, rows):
         at = part * hw + h * HEAD_DIM
@@ -565,11 +526,16 @@
     def beside(parts):
         return jnp.concatenate(parts, axis=1) if len(parts) > 1 else parts[0]
 
+    parts_o, wo = ref.wout_parts, ref.wo
+    wg = Gather(net, lambda rows: parts_o.at[:, rows], lambda i, rows: wo.at[:, i, rows], r)
+
+    def put(array, i, value):
+        array[2 * i], array[2 * i + 1] = value[:R], value[R:]
+
     for i in range(tiles):
         if i == tiles - 2:
             zo.wait()
-            route.start()
-            zu.relay()
+            wg.begin()
             load_d.wait()
             zd.begin()
         n = (i + 1) * step
@@ -584,31 +550,29 @@
             total = jnp.sum(e, axis=1, keepdims=True)
             parts.append((mm(e.astype(bf16), head(2, h, keys), NN) / total).astype(bf16))
             lse[h, rows, :] = top + jnp.log(total)
-        mix[rows, :] = beside(parts)
-    gc.finish()
-    route.wait()
-    w_out = ref["wout"][...].reshape(hw, D)
-
-    def reducer(k):
-        return Reduce(
-            net, ref["sib_send"], ref["sib_recv"].at[k % 2], ref["far_send"], ref["far_recv"].at[k % 2],
-            ref["keep"],
-        )
-
-    red = reducer(0)
-    red.begin(lambda chip: mm(mix[tile(chip), :], w_out, NN))
-    zd.relay()
-    total = red.finish()
-    resid = xs[c].astype(f32) + total + vectors.get("out")
+        put(mix, i, beside(parts))
+    swap_mix = Swap(net, mix, ref.mixf)
+    swap_mix.start()
+    wg.middle()
+    wo[:, c] = parts_o[...]
+    zu.relay()
+    swap_mix.wait()
+    wg.finish()
+    w_out = wo[...].reshape(D, D)
+    mixed = jnp.concatenate([ref.mixf[i] for i in range(C)], axis=1)
+    x_own = xs[c]
+    ref.x_own[...] = x_own
+    resid = x_own.astype(f32) + mm(mixed, w_out, NN) + vectors.get("out")
     xhat2, scale2 = row_stats(resid)
     gain2 = vectors.get("gain2")
     n2[c] = (xhat2 * gain2 + vectors.get("shift2")).astype(bf16)
-    ref["resid"][...] = resid
-    gn = Gather(net, n2.at[c], n2)
+    ref.resid[...] = resid
+    gn = tokens(n2.at[c], n2)
     gn.begin()
     gn.middle()
+    zd.relay()
     zu.wait()
-    w_up = ref["wup"][...].reshape(D, fw)
+    w_up = ref.wup[...].reshape(D, fw)
     up = vectors.get("up")
     b_up = jnp.concatenate(
         [
@@ -618,22 +582,16 @@
         axis=1,
     )
     gn.finish()
-    zd.wait()
-    w_down = ref["wdown"][...].reshape(fw, D)
-    hid, pg = ref["hid"], ref["pg"]
-
-    def feed(i, sums):
+    hid, pg, slopes = ref.hid, ref.pg, ref.slopes
+
+    def feed(i, carry):
         rows = tile(i)
         value, slope = gelu_both(mm(blocks(n2, i), w_up, NN) + b_up)
         hid[rows, :] = value.astype(bf16)
-        grad = (mm(blocks(cot, i), w_down, NT) * slope).astype(bf16)
-        pg[rows, :] = grad
-        return sums + column_sum(grad.astype(f32))
-
-    up_sums = lax.fori_loop(0, tiles, feed, jnp.zeros((1, fw), f32))
-
-    red = reducer(1)
-    red.begin(lambda chip: mm(pg[tile(chip), :], w_up, NT))
+        slopes[rows, :] = slope
+        return carry
+
+    lax.fori_loop(0, tiles, feed, 0)
 
     lanes = 128
 
@@ -643,17 +601,33 @@
     def chunk(i):
         return pl.ds(pl.multiple_of(i * lanes, lanes), lanes)
 
-    dbuf, ubuf, obuf, qbuf = (ref[k] for k in ("dbuf", "ubuf", "obuf", "qbuf"))
+    dbuf, ubuf, obuf, qbuf = (ref.dbuf, ref.ubuf, ref.obuf, ref.qbuf)
 
     def down_part(i, carry):
         dbuf[chunk(i), :] = mm(hid[:, chunk(i)], whole(cot), TN).astype(bf16)
         return carry
 
     lax.fori_loop(0, fw // lanes, down_part, 0)
+    zd.wait()
     rd = ZReduce(
-        net, lambda zs: dbuf.at[pl.ds(pl.multiple_of(zs * fzc, fzc), fzc)], ref["drecv"], ref["dsum"]
+        net, lambda zs: dbuf.at[pl.ds(pl.multiple_of(zs * fzc, fzc), fzc)], ref.drecv, ref.dsum
     )
     rd.begin()
+    w_down = ref.wdown[...].reshape(fw, D)
+
+    up_sums = []
+
+    def feed_back(chip):
+        rows = tile(chip)
+        grad = (mm(blocks(cot, chip), w_down, NT) * slopes[rows, :]).astype(bf16)
+        pg[rows, :] = grad
+        up_sums.append(column_sum(grad.astype(f32)))
+        return mm(grad, w_up, NT)
+
+    sib_recv, far_recv = ref.sib_recv, ref.far_recv
+    red = Reduce(net, ref.sib_send, sib_recv.at[0], ref.far_send, far_recv.at[0], ref.keep)
+    red.begin(feed_back)
+    up_sums = sum(up_sums)
     per = lanes // (Z * r)
 
     def up_part(i, carry):
@@ -662,17 +636,23 @@
         return carry
 
     lax.fori_loop(0, D // lanes, up_part, 0)
-    ru = ZReduce(net, lambda zs: ubuf.at[:, zs], ref["urecv"], ref["usum"])
+    ru = ZReduce(net, lambda zs: ubuf.at[:, zs], ref.urecv, ref.usum)
     ru.begin()
 
     n2_grad = red.finish()
     cot_own = cot[c].astype(f32)
-    xhat2, scale2 = row_stats(ref["resid"][...])
+    xhat2, scale2 = row_stats(ref.resid[...])
     resid_grad = cot_own + norm_back(n2_grad, xhat2, scale2, gain2)
     branch = resid_grad.astype(bf16)
     bg[c] = branch
-    ref["rgrad"][...] = resid_grad
-    gb = Gather(net, bg.at[c], bg)
+    ref.rgrad[...] = resid_grad
+    back = mm(branch, w_out, NT).astype(bf16)
+    mg = ref.mg
+    for i in range(C):
+        ref.mixf[i] = back[:, i * hw : (i + 1) * hw]
+    swap_mg = Swap(net, ref.mixf, mg)
+    swap_mg.start()
+    gb = tokens(bg.at[c], bg)
     gb.begin()
     sums = {
         "out": column_sum(branch.astype(f32)),
@@ -680,69 +660,36 @@
         "shift2": column_sum(n2_grad),
         "down": column_sum(cot_own),
     }
-    mg = ref["mg"]
-
-    def back_out(d):
-        block = c ^ d
-        rows = pl.ds(pl.multiple_of(block * R, R), R)
-        mg[rows, :] = mm(bg[block], w_out, NT).astype(bf16)
-
-    back_out(0)
-    gb.middle()
-    rd.relay()
-    gb.finish(back_out)
-    obuf[...] = mm(mix[...], whole(bg), TN).astype(bf16)
-    ro = ZReduce(
-        net, lambda zs: obuf.at[pl.ds(pl.multiple_of(zs * r, r), r)], ref["orecv"], ref["osum"]
-    )
-    ro.begin()
-    red = reducer(2)
-    red.begin(lambda chip: mm(hid[tile(chip), :], w_down, NN))
-
-    qg, dk, dv = ref["qg"], ref["dk"], ref["dv"]
-    dk[...] = jnp.zeros((S, hw), f32)
-    dv[...] = jnp.zeros((S, hw), f32)
-    swap_up = Swap(net, ref["uparts"], ref["ufrom"])
+    swap_mg.wait()
+    qg, dkv = ref.qg, ref.dkv
+    dkv[...] = jnp.zeros((S, 2 * hw), f32)
+    swap_up = Swap(net, ref.uparts, ref.ufrom)
     for i in range(tiles):
         n = (i + 1) * step
         rows, keys = slice(i * step, n), slice(0, n)
+        if i == 1:
+            gb.middle()
+        if i == tiles - 1:
+            rd.relay()
+            ru.relay()
         allowed = masked(i)
+        g_rows = mg[2 * i : 2 * i + 2].reshape(step, hw)
+        m_rows = mix[2 * i : 2 * i + 2].reshape(step, hw)
         dqs, dks, dvs = [], [], []
         for h in range(heads):
             at = h * HEAD_DIM
             q, k, v = head(0, h, rows), head(1, h, keys), head(2, h, keys)
-            g = mg[rows, at : at + HEAD_DIM]
-            m = mix[rows, at : at + HEAD_DIM]
+            g, m = g_rows[:, at : at + HEAD_DIM], m_rows[:, at : at + HEAD_DIM]
             s = mm(q, k, NT) * score_scale - lse[h, rows, :]
             p = jnp.where(allowed, jnp.exp(s), 0.0)
             delta = jnp.sum(g.astype(f32) * m.astype(f32), axis=1, keepdims=True)
             ds = (p * (mm(g, v, NT) - delta)).astype(bf16)
             dqs.append(score_scale * mm(ds, k, NN))
-            dks.append(mm(ds, q, TN))
+            dks.append(score_scale * mm(ds, q, TN))
             dvs.append(mm(p.astype(bf16), g, TN))
         qg[rows, 0:hw] = beside(dqs).astype(bf16)
-        dk[keys, :] += beside(dks)
-        dv[keys, :] += beside(dvs)
-        if i == tiles - 3:
-            ref["hbuf"][...] = rd.total().astype(bf16)
-            there = net.to(net.home, ref["hbuf"], ref["hrecv"], net.take(1), net.used - 1)
-            here = pltpu.make_async_copy(ref["hbuf"], ref["hrecv"], local.at[0])
-
-            @pl.when(net.at_home)
-            def _():
-                here.start()
-
-            @pl.when(jnp.logical_not(net.at_home))
-            def _():
-                there.start()
-
-            ru.relay()
-        if i == tiles - 2:
-            total = red.finish()
-            ref["layer_out"][...] = (ref["resid"][...] + total + vectors.get("down")).astype(bf16)
-            ro.relay()
-    qg[:, hw : 2 * hw] = (score_scale * dk[...]).astype(bf16)
-    qg[:, 2 * hw : 3 * hw] = dv[...].astype(bf16)
+        dkv[keys, :] += beside(dks + dvs)
+    qg[:, hw : 3 * hw] = dkv[...].astype(bf16)
 
     def qkv_part(i, carry):
         grad = mm(n1[:, :, chunk(i)].reshape(S, lanes), qg[...], TN).astype(bf16)
@@ -750,34 +697,57 @@
         return carry
 
     lax.fori_loop(0, D // lanes, qkv_part, 0)
-    rq = ZReduce(net, lambda zs: qbuf.at[:, zs], ref["qrecv"], ref["qsum"])
+    rq = ZReduce(net, lambda zs: qbuf.at[:, zs], ref.qrecv, ref.qsum)
     rq.begin()
-    red = reducer(3)
+    red = Reduce(net, ref.sib_send, sib_recv.at[1], ref.far_send, far_recv.at[1], ref.keep)
     red.begin(lambda chip: mm(qg[tile(chip), :], w_qkv, NT))
+    gb.finish()
+    obuf[...] = mm(mix[...].reshape(S, hw), whole(bg), TN).astype(bf16)
+    ro = ZReduce(
+        net, lambda zs: obuf.at[pl.ds(pl.multiple_of(zs * r, r), r)], ref.orecv, ref.osum
+    )
+    ro.begin()
     qkv_sums = column_sum(qg[...].astype(f32))
-    ref["uparts"][...] = ru.total().astype(bf16)
-    swap_up.start()
-    ref["d_out"][...] = ro.total()
-    colz, colp = ref["colz"], ref["colp"]
+    colz, colp = ref.colz, ref.colp
     colz[z] = jnp.concatenate([qkv_sums[:, 0:hw], qkv_sums[:, 2 * hw : 3 * hw], up_sums], axis=1)
     line = Spread(net, colz, False)
     line.start()
 
+    n1_grad = red.finish()
+    red_out = Reduce(net, ref.sib_send, sib_recv.at[0], ref.far_send, far_recv.at[0], ref.keep)
+    red_out.begin(lambda chip: mm(hid[tile(chip), :], w_down, NN))
+    xhat1, scale1 = row_stats(ref.x_own[...].astype(f32))
+    ref.input_grad[...] = (ref.rgrad[...] + norm_back(n1_grad, xhat1, scale1, gain1)).astype(bf16)
+    stack = jnp.concatenate(
+        [
+            column_sum(n1_grad * xhat1), column_sum(n1_grad), sums["out"], sums["gain2"],
+            sums["shift2"], sums["down"], jnp.zeros((2, D), f32),
+        ],
+        axis=0,
+    )
+    w = D // C
+    for i in range(C):
+        ref.tok_to[i] = stack[:, i * w : (i + 1) * w]
+    swap_tok = Swap(net, ref.tok_to, ref.tok_from)
+    swap_tok.start()
+    rq.relay()
+    ro.relay()
+
+    ref.dparts[...] = rd.total().astype(bf16)
+    home = net.take(1)
+    there = net.to(net.home, ref.dparts, ref.dfrom, home, home)
+    here = pltpu.make_async_copy(ref.dparts, ref.dfrom, local.at[0])
+
     @pl.when(net.at_home)
     def _():
-        here.wait()
+        here.start()
 
     @pl.when(jnp.logical_not(net.at_home))
     def _():
-        there.wait()
-
-    ref["d_down"][...] = ref["hrecv"][...].astype(f32)
-    swap_up.wait()
-    for i in range(C):
-        for q in range(Z):
-            ref["d_up"][:, (q * C + i) * fzc : (q * C + i + 1) * fzc] = ref["ufrom"][
-                i, :, q * fzc : (q + 1) * fzc
-            ].astype(f32)
+        there.start()
+
+    ref.uparts[...] = ru.total().astype(bf16)
+    swap_up.start()
     line.wait()
     total = colz[0]
     for i in range(1, Z):
@@ -785,49 +755,87 @@
     colp[c] = total
     plane = Spread(net, colp, True)
     plane.start()
-    rq.relay()
-    n1_grad = red.finish()
-    xhat1, scale1 = row_stats(xs[c].astype(f32))
-    ref["input_grad"][...] = (
-        ref["rgrad"][...] + norm_back(n1_grad, xhat1, scale1, gain1)
-    ).astype(bf16)
-    stack = jnp.concatenate(
-        [
-            column_sum(n1_grad * xhat1), column_sum(n1_grad), sums["out"], sums["gain2"],
-            sums["shift2"], sums["down"], jnp.zeros((2, D), f32),
-        ],
-        axis=0,
-    )
-    w = D // C
-    for i in range(C):
-        ref["tok_to"][i] = stack[:, i * w : (i + 1) * w]
-    swap_tok = Swap(net, ref["tok_to"], ref["tok_from"])
-    swap_tok.start()
-    ref["qparts"][...] = rq.total().astype(bf16)
-    swap_q = Swap(net, ref["qparts"], ref["qfrom"])
-    swap_q.start()
     swap_tok.wait()
-    tokz = ref["tokz"]
-    total = ref["tok_from"][0]
+    tokz = ref.tokz
+    total = ref.tok_from[0]
     for i in range(1, C):
-        total = total + ref["tok_from"][i]
+        total = total + ref.tok_from[i]
     tokz[z] = total
     tok_line = Spread(net, tokz, False)
     tok_line.start()
-    swap_q.wait()
+
+    @pl.when(net.at_home)
+    def _():
+        here.wait()
+
+    @pl.when(jnp.logical_not(net.at_home))
+    def _():
+        there.wait()
+
+    ref.d_down[...] = ref.dfrom[...].astype(f32)
+    swap_up.wait()
     for i in range(C):
-        for p in range(3):
-            ref["d_qkv"][:, p * D + i * hw : p * D + (i + 1) * hw] = ref["qfrom"][
-                i, :, p * hw : (p + 1) * hw
+        for q in range(Z):
+            ref.d_up[:, (q * C + i) * fzc : (q * C + i + 1) * fzc] = ref.ufrom[
+                i, :, q * fzc : (q + 1) * fzc
             ].astype(f32)
+    ref.qparts[...] = rq.total().astype(bf16)
+    swap_q = Swap(net, ref.qparts, ref.qfrom)
+    swap_q.start()
+    ref.d_out[...] = ro.total()
     tok_line.wait()
     total = tokz[0]
     for i in range(1, Z):
         total = total + tokz[i]
-    ref["tok"][...] = total
+    ref.tok[...] = chosen([total[:, i * r : (i + 1) * r] for i in range(Z)], z)
+    total = red_out.finish()
+    ref.layer_out[...] = (ref.resid[...] + total + vectors.get("down")).astype(bf16)
     plane.wait()
+    mine = c * Z + z
+    part = D * 2 // (C * Z)
+
+    def piece(at, size):
+        rest, row = at % hw, (at % D) // hw
+        start = hw * (at // D) + rest
+        return colp[row, :, start : start + size]
+
+    ref.qv[...] = chosen([piece(i * part, part) for i in range(C * Z)], mine)
+    ref.up[...] = chosen(
+        [
+            colp[i, :, 2 * hw + q * fzc : 2 * hw + (q + 1) * fzc]
+            for q in range(Z)
+            for i in range(C)
+        ],
+        mine,
+    )
+    swap_q.wait()
+    for i in range(C):
+        for p in range(3):
+            ref.d_qkv[:, p * D + i * hw : p * D + (i + 1) * hw] = ref.qfrom[
+                i, :, p * hw : (p + 1) * hw
+            ].astype(f32)
+    assert net.used <= ref.sems.shape[1]
     for part in (zv, zq, zo, zu, zd, rd, ru, ro, rq):
         part.finish()
+
+
+def hand_over(count, *refs):
+    big, (tok, qv, up) = refs[:count], refs[count : count + 3]
+    rest, sems = refs[count + 3 :], refs[-1]
+    outs, held = rest[: count + 8], rest[count + 8 : -1]
+    into = [pltpu.make_async_copy(big[i], held[i], sems.at[0, i]) for i in range(count)]
+    out = [pltpu.make_async_copy(held[i], outs[i], sems.at[1, i]) for i in range(count)]
+    for copy in into:
+        copy.start()
+    for i in range(6):
+        outs[count + i][...] = tok[i : i + 1, :]
+    outs[count + 6][...] = qv[...]
+    outs[count + 7][...] = up[...]
+    for i in range(count):
+        into[i].wait()
+        out[i].start()
+    for copy in out:
+        copy.wait()
 
 
 def shards(
@@ -859,7 +867,11 @@
     )
     sizes = tuple(v.shape[0] for v in all_vectors)
     V, W = sum(sizes), 2 * hw + fw
-    vec_in = jnp.concatenate(all_vectors).astype(f32)[None]
+    vec_in, at = jnp.zeros((V,), f32), 0
+    for v in all_vectors:
+        vec_in = vec_in + jnp.pad(v.astype(f32), (at, V - at - v.shape[0]))
+        at += v.shape[0]
+    vec_in = vec_in[None]
     aligned = hw % 128 == 0 and fzc % 128 == 0
     wqkv_in, wup_in = qkv_weight, up_weight
     if not aligned:
@@ -871,71 +883,77 @@
         ).reshape(D // Z, fw)
 
     vmem, hbm = pltpu.VMEM, pl.BlockSpec(memory_space=pl.ANY)
-    ins = {
-        "x_in": (tokens_in[0], hbm),
-        "cot_in": (out_cotangent[0], hbm),
-        "docs": (doc_lengths, pl.BlockSpec(memory_space=pltpu.SMEM)),
-        "vec_in": (vec_in, hbm),
-        "wqkv_in": (wqkv_in, hbm),
-        "wout_in": (out_weight, hbm),
-        "wup_in": (wup_in, hbm),
-        "wdown_in": (down_weight, hbm),
-    }
-    outs = {
-        "layer_out": ((R, D), bf16),
-        "input_grad": ((R, D), bf16),
-        "d_qkv": ((r, 3 * D), f32),
-        "d_out": ((r, D), f32),
-        "d_up": ((r, ff), f32),
-        "d_down": ((fzc, D), f32),
-        "tok": ((8, D // C), f32),
-        "colp": ((C, 1, W), f32),
-    }
+    ins = dict(
+        x_in=(tokens_in[0], hbm),
+        cot_in=(out_cotangent[0], hbm),
+        docs=(doc_lengths, pl.BlockSpec(memory_space=pltpu.SMEM)),
+        vec_in=(vec_in, hbm),
+        wqkv_in=(wqkv_in, hbm),
+        wout_in=(out_weight, hbm),
+        wup_in=(wup_in, hbm),
+        wdown_in=(down_weight, hbm),
+    )
+    outs = dict(
+        layer_out=((R, D), bf16),
+        input_grad=((R, D), bf16),
+        d_qkv=((r, 3 * D), f32),
+        d_out=((r, D), f32),
+        d_up=((r, ff), f32),
+        d_down=((fzc, D), f32),
+        tok=((8, r), f32),
+        qv=((1, 2 * r), f32),
+        up=((1, fzc), f32),
+    )
     token, own = (C, R, D), (R, D)
-    exchange = {"far_send": bf16, "sib_send": bf16, "keep": f32}
-    scratch = {
-        **{k: (token, bf16) for k in ("xs", "n1", "n2", "cot", "bg")},
-        "qkv": ((S, 3 * hw), bf16),
-        "qg": ((S, 3 * hw), bf16),
-        "mix": ((S, hw), bf16),
-        "mg": ((S, hw), bf16),
-        "lse": ((heads, S, 1), f32),
-        "dk": ((S, hw), f32),
-        "dv": ((S, hw), f32),
-        "hid": ((S, fw), bf16),
-        "pg": ((S, fw), bf16),
-        "resid": (own, f32),
-        "rgrad": (own, f32),
-        "vec": ((Z, 1, V), f32),
-        "wqkv": ((Z, D // Z, 3 * hw), bf16),
-        "wout_parts": ((Z, r, D), bf16),
-        "wout": ((Z, r, D), bf16),
-        "wup": ((Z, D // Z, fw), bf16),
-        "wdown": ((Z, fzc, D), bf16),
-        "first": ((S, 1), jnp.int32),
-        **{k: ((chips, R, D), t) for k, t in exchange.items()},
-        "sib_recv": ((2, chips, R, D), bf16),
-        "far_recv": ((2, chips, R, D), bf16),
-        "dbuf": ((fw, D), bf16),
-        "ubuf": ((C, Z, r, fw), bf16),
-        "obuf": ((hw, D), bf16),
-        "qbuf": ((C, Z, r, 3 * hw), bf16),
-        "hbuf": ((fzc, D), bf16),
-        "hrecv": ((fzc, D), bf16),
-        "colz": ((Z, 1, W), f32),
-        "tok_to": ((C, 8, D // C), f32),
-        "tok_from": ((C, 8, D // C), f32),
-        "tokz": ((Z, 8, D // C), f32),
-    }
-    shard = {"d": (fzc, D), "u": (C, r, fw), "o": (r, D), "q": (C, r, 3 * hw)}
+    scratch = dict(
+        xs=(token, bf16),
+        n1=(token, bf16),
+        n2=(token, bf16),
+        cot=(token, bf16),
+        qkv=((S, 3 * hw), bf16),
+        qg=((S, 3 * hw), bf16),
+        mix=((C, R, hw), bf16),
+        mixf=((C, R, hw), bf16),
+        mg=((C, R, hw), bf16),
+        slopes=((S, fw), f32),
+        wo=((Z, C, r, D), bf16),
+        lse=((heads, S, 1), f32),
+        dkv=((S, 2 * hw), f32),
+        hid=((S, fw), bf16),
+        pg=((S, fw), bf16),
+        x_own=(own, bf16),
+        resid=(own, f32),
+        rgrad=(own, f32),
+        vec=((Z, 1, V), f32),
+        wqkv=((Z, D // Z, 3 * hw), bf16),
+        wout_parts=((Z, r, D), bf16),
+        wup=((Z, D // Z, fw), bf16),
+        wdown=((Z, fzc, D), bf16),
+        first=((S, 1), jnp.int32),
+        sib_send=((chips, R, D), bf16),
+        far_send=((chips, R, D), bf16),
+        keep=((chips, R, D), f32),
+        sib_recv=((2, chips, R, D), bf16),
+        far_recv=((2, chips, R, D), bf16),
+        dbuf=((fw, D), bf16),
+        ubuf=((C, Z, r, fw), bf16),
+        obuf=((hw, D), bf16),
+        qbuf=((C, Z, r, 3 * hw), bf16),
+        colz=((Z, 1, W), f32),
+        tok_to=((C, 8, D // C), f32),
+        tok_from=((C, 8, D // C), f32),
+        colp=((C, 1, W), f32),
+        tokz=((Z, 8, D // C), f32),
+    )
+    shard = dict(d=(fzc, D), u=(C, r, fw), o=(r, D), q=(C, r, 3 * hw))
     for k, shape in shard.items():
         scratch[k + "recv"] = ((Z - 1, *shape), bf16)
         scratch[k + "sum"] = ((Z // 2, *shape), bf16)
-    for k in ("u", "q"):
-        scratch[k + "parts"] = (shard[k], bf16)
-        scratch[k + "from"] = (shard[k], bf16)
-    gathers = 4 * max(13, C)
-    count = gathers + 10 * Z + 8 * chips + 5 * C + 8
+        if k != "o":
+            scratch[k + "parts"] = (shape, bf16)
+            scratch[k + "from"] = (shape, bf16)
+    gathers = 5 * max(13, C)
+    count = gathers + 12 * Z + 6 * chips + 6 * C + 2
     names = (*ins, *outs, *scratch, "sems", "local")
     got = pl.pallas_call(
         functools.partial(layer_kernel, names, chips, Z, sizes, aligned),
@@ -949,28 +967,21 @@
         ),
         name="layer",
     )(*[v[0] for v in ins.values()])
-    got = dict(zip(outs, got))
-
-    mine = c * Z + z
-    tok = lax.dynamic_slice_in_dim(got["tok"], z * r, r, axis=1)
-    col = got["colp"][:, 0]
-    qv = jnp.concatenate([col[:, :hw].reshape(D), col[:, hw : 2 * hw].reshape(D)])
-    up = col[:, 2 * hw :].reshape(C, Z, fzc).transpose(1, 0, 2).reshape(C * Z, fzc)
+    big = 6
+    results = list(outs.values())[:big] + [((1, r), f32)] * 6 + [outs[k] for k in list(outs)[-2:]]
+    done = pl.pallas_call(
+        functools.partial(hand_over, big),
+        out_shape=[jax.ShapeDtypeStruct(*v) for v in results],
+        in_specs=[hbm] * big + [pl.BlockSpec(memory_space=vmem)] * 3,
+        out_specs=[hbm] * big + [pl.BlockSpec(memory_space=vmem)] * 8,
+        scratch_shapes=[vmem(*v) for v in results[:big]] + [pltpu.SemaphoreType.DMA((2, big))],
+        name="hand_over",
+    )(*got)
+    layer_out, input_grad, d_qkv, d_out, d_up, d_down = done[:big]
+    gain1, shift1, out, gain2, shift2, down, qv, up = (v.reshape(-1) for v in done[big:])
     return (
-        got["layer_out"][None],
-        got["input_grad"][None],
-        tok[0],
-        tok[1],
-        got["d_qkv"],
-        lax.dynamic_index_in_dim(qv.reshape(C * Z, -1), mine, keepdims=False),
-        got["d_out"],
-        tok[2],
-        tok[3],
-        tok[4],
-        got["d_up"],
-        lax.dynamic_index_in_dim(up, mine, keepdims=False),
-        got["d_down"],
-        tok[5],
+        layer_out[None], input_grad[None], gain1, shift1, d_qkv, qv, d_out, out,
+        gain2, shift2, d_up, up, d_down, down,
     )
 
 

time: 186 us -> 163 us (0.88)
  local copies, waits for them, and re-layouts: 15.5 us -> 0 us
  Pallas kernels: 169 us -> 160 us
    unnamed x20 -> x0, local copies, waits for them, and re-layouts: 12.8 us -> none
    pallas_call x1, Pallas kernels: 169 us -> 157 us  [shards(): pl.pallas_call(functools.partial(layer_kernel, names, chips, Z, sizes, al...]
    pallas_call x0 -> x1, Pallas kernels: none -> 3.68 us  [shards(): pl.pallas_call(functools.partial(hand_over, big), out_shape=[jax.ShapeDty...]
where the time goes in v1:
time: 163 us; the launch traced here: 162 us
  Pallas kernels  160 us (98%)
    pallas_call x1, Pallas kernels, shards(): pl.pallas_call(functools.partial(layer_kernel, names, chips, Z, sizes, al...  157 us
    pallas_call x1, Pallas kernels, shards(): pl.pallas_call(functools.partial(hand_over, big), out_shape=[jax.ShapeDty...  3.68 us

profile of v1, /device:TPU:0, one launch (start us, length us, event | category | flops | bytes accessed | tf_op | source)
XLA Modules:
  0.0 162.5 jit_solution(7185236408146034559)
XLA Ops:
  0.6 1.4 convert_add_fusion
  2.0 156.6 %layer.1 = (bf16[128,1024]{1,0:T(8,128)(2,1)}, bf16[128,1024]{1,0:T(8,128)(2,1)}, f32[32,3072]{1,0:T(8,128)}, f32[32,1024]{1,0:T(8,128)}, f32[32,4096]{1,0:T(8,1...) custom-call(bf16[128,1024]{1,0:T(8,128)(2,1)} %bitcast.13, ...), custom_call_target="tpu_custom_call" | custom-call | tf_op jit(solution)/shard_map/layer/pallas_call | solution.py:958
  158.6 3.7 %hand_over.1 = (bf16[128,1024]{1,0:T(8,128)(2,1)}, bf16[128,1024]{1,0:T(8,128)(2,1)}, f32[32,3072]{1,0:T(8,128)}, f32[32,1024]{1,0:T(8,128)}, f32[32,4096]{1,0:T...) custom-call(bf16[128,1024]{1,0:T(8,128)(2,1)} %get-tuple-element.37., ...), custom_call_target="tpu_custom_call" | custom-call | tf_op jit(solution)/shard_map/hand_over/pallas_call | solution.py:972

commit v2 on v1

--- a/solution.py
+++ b/solution.py
@@ -72,11 +72,12 @@
         self.c = lax.axis_index("ctx")
         self.z = lax.axis_index("fsdp")
         self.sems, self.used = sems, 0
-        block = self.z * self.C + self.c
-        self.home = (block // Z, block % Z)
-        mine = self.c * Z + self.z
-        self.origin = (mine % self.C, mine // self.C)
-        self.at_home = block == mine
+        q = self.z ^ (self.c % Z)
+        self.home = q * (self.C // Z) + self.c // Z
+        self.at_home = self.home == self.c
+
+    def block(self, q, c):
+        return self.Z * (c // self.Z) + (q ^ (c % self.Z))
 
     def take(self, count):
         self.used += count
@@ -89,12 +90,7 @@
         for peer in peers:
             pl.semaphore_signal(sem, inc=1, device_id=peer, device_id_type=MESH)
 
-        @pl.when(jnp.logical_not(self.at_home))
-        def _():
-            for peer in (self.home, self.origin):
-                pl.semaphore_signal(sem, inc=1, device_id=peer, device_id_type=MESH)
-
-        pl.semaphore_wait(sem, len(peers) + jnp.where(self.at_home, 0, 2))
+        pl.semaphore_wait(sem, len(peers))
 
     def to(self, device, src, dst, out, into):
         return pltpu.make_async_remote_copy(
@@ -425,7 +421,7 @@
         FZ = fzc * C
         load_u = [
             bring(
-                ref.wup_in.at[:, pl.ds(pl.multiple_of(p * FZ + c * fzc, fzc), fzc)],
+                ref.wup_in.at[:, pl.ds(pl.multiple_of(p * FZ + net.block(p, c) * fzc, fzc), fzc)],
                 ref.wup.at[z, :, p * fzc : (p + 1) * fzc], 8 + p,
             )
             for p in range(Z)
@@ -434,7 +430,7 @@
         load_q = [bring(ref.wqkv_in, ref.wqkv.at[z], 2)]
         load_u = [bring(ref.wup_in, ref.wup.at[z], 8)]
     load_o = bring(ref.wout_in.at[pl.ds(pl.multiple_of(c * r, r), r)], ref.wout_parts.at[z], 5)
-    load_d = bring(ref.wdown_in.at[pl.ds(pl.multiple_of(c * fzc, fzc), fzc)], ref.wdown.at[z], 6)
+    load_d = bring(ref.wdown_in.at[pl.ds(pl.multiple_of(net.block(z, c) * fzc, fzc), fzc)], ref.wdown.at[z], 6)
     load_c = bring(cot_in, cot.at[c], 7)
 
     zv, zq = ZGather(net, ref.vec), ZGather(net, ref.wqkv)
@@ -533,9 +529,11 @@
         array[2 * i], array[2 * i + 1] = value[:R], value[R:]
 
     for i in range(tiles):
-        if i == tiles - 2:
+        if i == 1:
             zo.wait()
             wg.begin()
+        if i == tiles - 1:
+            wg.middle()
             load_d.wait()
             zd.begin()
         n = (i + 1) * step
@@ -553,7 +551,6 @@
         put(mix, i, beside(parts))
     swap_mix = Swap(net, mix, ref.mixf)
     swap_mix.start()
-    wg.middle()
     wo[:, c] = parts_o[...]
     zu.relay()
     swap_mix.wait()
@@ -576,7 +573,10 @@
     up = vectors.get("up")
     b_up = jnp.concatenate(
         [
-            chosen([up[:, (q * C + i) * fzc : (q * C + i + 1) * fzc] for i in range(C)], c)
+            chosen(
+                [up[:, (q * C + i) * fzc : (q * C + i + 1) * fzc] for i in range(C)],
+                net.block(q, c),
+            )
             for q in range(Z)
         ],
         axis=1,
@@ -610,7 +610,10 @@
     lax.fori_loop(0, fw // lanes, down_part, 0)
     zd.wait()
     rd = ZReduce(
-        net, lambda zs: dbuf.at[pl.ds(pl.multiple_of(zs * fzc, fzc), fzc)], ref.drecv, ref.dsum
+        net,
+        lambda zs: dbuf.at[pl.ds(pl.multiple_of((zs ^ (c % Z)) * fzc, fzc), fzc)],
+        ref.drecv,
+        ref.dsum,
     )
     rd.begin()
     w_down = ref.wdown[...].reshape(fw, D)
@@ -661,6 +664,7 @@
         "down": column_sum(cot_own),
     }
     swap_mg.wait()
+    rd.relay()
     qg, dkv = ref.qg, ref.dkv
     dkv[...] = jnp.zeros((S, 2 * hw), f32)
     swap_up = Swap(net, ref.uparts, ref.ufrom)
@@ -670,7 +674,6 @@
         if i == 1:
             gb.middle()
         if i == tiles - 1:
-            rd.relay()
             ru.relay()
         allowed = masked(i)
         g_rows = mg[2 * i : 2 * i + 2].reshape(step, hw)
@@ -707,12 +710,27 @@
         net, lambda zs: obuf.at[pl.ds(pl.multiple_of(zs * r, r), r)], ref.orecv, ref.osum
     )
     ro.begin()
+    ref.dparts[...] = rd.total().astype(bf16)
+    home = net.take(1)
+    there = net.to((net.home, z), ref.dparts, ref.dfrom, home, home)
+    here = pltpu.make_async_copy(ref.dparts, ref.dfrom, local.at[0])
+
+    @pl.when(net.at_home)
+    def _():
+        here.start()
+
+    @pl.when(jnp.logical_not(net.at_home))
+    def _():
+        there.start()
+
     qkv_sums = column_sum(qg[...].astype(f32))
     colz, colp = ref.colz, ref.colp
     colz[z] = jnp.concatenate([qkv_sums[:, 0:hw], qkv_sums[:, 2 * hw : 3 * hw], up_sums], axis=1)
     line = Spread(net, colz, False)
     line.start()
 
+    ref.uparts[...] = ru.total().astype(bf16)
+    swap_up.start()
     n1_grad = red.finish()
     red_out = Reduce(net, ref.sib_send, sib_recv.at[0], ref.far_send, far_recv.at[0], ref.keep)
     red_out.begin(lambda chip: mm(hid[tile(chip), :], w_down, NN))
@@ -733,21 +751,6 @@
     rq.relay()
     ro.relay()
 
-    ref.dparts[...] = rd.total().astype(bf16)
-    home = net.take(1)
-    there = net.to(net.home, ref.dparts, ref.dfrom, home, home)
-    here = pltpu.make_async_copy(ref.dparts, ref.dfrom, local.at[0])
-
-    @pl.when(net.at_home)
-    def _():
-        here.start()
-
-    @pl.when(jnp.logical_not(net.at_home))
-    def _():
-        there.start()
-
-    ref.uparts[...] = ru.total().astype(bf16)
-    swap_up.start()
     line.wait()
     total = colz[0]
     for i in range(1, Z):
@@ -776,9 +779,8 @@
     swap_up.wait()
     for i in range(C):
         for q in range(Z):
-            ref.d_up[:, (q * C + i) * fzc : (q * C + i + 1) * fzc] = ref.ufrom[
-                i, :, q * fzc : (q + 1) * fzc
-            ].astype(f32)
+            at = (q * C + net.block(q, i)) * fzc
+            ref.d_up[:, at : at + fzc] = ref.ufrom[i, :, q * fzc : (q + 1) * fzc].astype(f32)
     ref.qparts[...] = rq.total().astype(bf16)
     swap_q = Swap(net, ref.qparts, ref.qfrom)
     swap_q.start()
@@ -802,7 +804,7 @@
     ref.qv[...] = chosen([piece(i * part, part) for i in range(C * Z)], mine)
     ref.up[...] = chosen(
         [
-            colp[i, :, 2 * hw + q * fzc : 2 * hw + (q + 1) * fzc]
+            colp[net.block(q, i), :, 2 * hw + q * fzc : 2 * hw + (q + 1) * fzc]
             for q in range(Z)
             for i in range(C)
         ],
@@ -878,9 +880,16 @@
         wqkv_in = lax.dynamic_index_in_dim(
             qkv_weight.reshape(D // Z, 3, C, hw), c, axis=2, keepdims=False
         ).reshape(D // Z, 3 * hw)
-        wup_in = lax.dynamic_index_in_dim(
-            up_weight.reshape(D // Z, Z, C, fzc), c, axis=2, keepdims=False
-        ).reshape(D // Z, fw)
+        split = up_weight.reshape(D // Z, Z, C, fzc)
+        wup_in = jnp.concatenate(
+            [
+                lax.dynamic_index_in_dim(
+                    split[:, q], Z * (c // Z) + (q ^ (c % Z)), axis=1, keepdims=False
+                )
+                for q in range(Z)
+            ],
+            axis=1,
+        )
 
     vmem, hbm = pltpu.VMEM, pl.BlockSpec(memory_space=pl.ANY)
     ins = dict(

time: 163 us -> 154 us (0.945)
  Pallas kernels: 160 us -> 151 us
    pallas_call x1, Pallas kernels: 157 us -> 148 us  [shards(): pl.pallas_call(functools.partial(layer_kernel, names, chips, Z, sizes, al...]
where the time goes in v2:
time: 154 us
  Pallas kernels  151 us (98%)
    pallas_call x1, Pallas kernels, shards(): pl.pallas_call(functools.partial(layer_kernel, names, chips, Z, sizes, al...  148 us
    pallas_call x1, Pallas kernels, shards(): pl.pallas_call(functools.partial(hand_over, big), out_shape=[jax.ShapeDty...  3.68 us

profile of v2, /device:TPU:0, one launch (start us, length us, event | category | flops | bytes accessed | tf_op | source)
XLA Modules:
  0.0 153.6 jit_solution(16632285757971999254)
XLA Ops:
  0.6 1.4 convert_add_fusion
  2.0 147.7 %layer.1 = (bf16[128,1024]{1,0:T(8,128)(2,1)}, bf16[128,1024]{1,0:T(8,128)(2,1)}, f32[32,3072]{1,0:T(8,128)}, f32[32,1024]{1,0:T(8,128)}, f32[32,4096]{1,0:T(8,1...) custom-call(bf16[128,1024]{1,0:T(8,128)(2,1)} %bitcast.13, ...), custom_call_target="tpu_custom_call" | custom-call | tf_op jit(solution)/shard_map/layer/pallas_call | solution.py:967
  149.7 3.7 %hand_over.1 = (bf16[128,1024]{1,0:T(8,128)(2,1)}, bf16[128,1024]{1,0:T(8,128)(2,1)}, f32[32,3072]{1,0:T(8,128)}, f32[32,1024]{1,0:T(8,128)}, f32[32,4096]{1,0:T...) custom-call(bf16[128,1024]{1,0:T(8,128)(2,1)} %get-tuple-element.37., ...), custom_call_target="tpu_custom_call" | custom-call | tf_op jit(solution)/shard_map/hand_over/pallas_call | solution.py:981

commit v3 on v2

--- a/solution.py
+++ b/solution.py
@@ -445,6 +445,8 @@
 
     gx = tokens(x_in, xs)
     gx.begin()
+    load_o.wait()
+    zo.begin()
     for copy in load_q:
         copy.wait()
     zq.begin()
@@ -470,16 +472,16 @@
 
     norm_one(0)
     gx.middle()
+    zo.relay()
     zq.relay()
-    load_o.wait()
-    zo.begin()
+    gx.finish(norm_one)
+    parts_o, wo = ref.wout_parts, ref.wo
+    wg = Gather(net, lambda rows: parts_o.at[:, rows], lambda i, rows: wo.at[:, i, rows], r)
+    zo.wait()
+    wg.begin()
+    wo[:, c] = parts_o[...]
     for copy in load_u:
         copy.wait()
-    zu.begin()
-    load_c.wait()
-    gc = tokens(cot_in, cot)
-    gc.begin()
-    gx.finish(norm_one)
 
     qv = vectors.get("qv")
     bias = jnp.concatenate(
@@ -490,8 +492,9 @@
         ],
         axis=1,
     )
-    gc.middle()
     zq.wait()
+    zu.begin()
+    wg.middle()
     w_qkv = ref.wqkv[...].reshape(D, 3 * hw)
 
     def blocks(array, i):
@@ -505,8 +508,9 @@
         return carry
 
     lax.fori_loop(0, S // step, project, 0)
-    zo.relay()
-    gc.finish()
+    load_c.wait()
+    gc = tokens(cot_in, cot)
+    gc.begin()
     tiles = S // step
 
     def masked(i):
@@ -522,18 +526,12 @@
     def beside(parts):
         return jnp.concatenate(parts, axis=1) if len(parts) > 1 else parts[0]
 
-    parts_o, wo = ref.wout_parts, ref.wo
-    wg = Gather(net, lambda rows: parts_o.at[:, rows], lambda i, rows: wo.at[:, i, rows], r)
-
     def put(array, i, value):
         array[2 * i], array[2 * i + 1] = value[:R], value[R:]
 
     for i in range(tiles):
-        if i == 1:
-            zo.wait()
-            wg.begin()
         if i == tiles - 1:
-            wg.middle()
+            wg.finish()
             load_d.wait()
             zd.begin()
         n = (i + 1) * step
@@ -551,10 +549,9 @@
         put(mix, i, beside(parts))
     swap_mix = Swap(net, mix, ref.mixf)
     swap_mix.start()
-    wo[:, c] = parts_o[...]
+    gc.middle()
     zu.relay()
     swap_mix.wait()
-    wg.finish()
     w_out = wo[...].reshape(D, D)
     mixed = jnp.concatenate([ref.mixf[i] for i in range(C)], axis=1)
     x_own = xs[c]
@@ -564,6 +561,7 @@
     gain2 = vectors.get("gain2")
     n2[c] = (xhat2 * gain2 + vectors.get("shift2")).astype(bf16)
     ref.resid[...] = resid
+    gc.finish()
     gn = tokens(n2.at[c], n2)
     gn.begin()
     gn.middle()
@@ -699,11 +697,11 @@
         qbuf[pl.ds(i * per, per)] = grad.reshape(per, Z, r, 3 * hw)
         return carry
 
+    red = Reduce(net, ref.sib_send, sib_recv.at[1], ref.far_send, far_recv.at[1], ref.keep)
+    red.begin(lambda chip: mm(qg[tile(chip), :], w_qkv, NT))
     lax.fori_loop(0, D // lanes, qkv_part, 0)
     rq = ZReduce(net, lambda zs: qbuf.at[:, zs], ref.qrecv, ref.qsum)
     rq.begin()
-    red = Reduce(net, ref.sib_send, sib_recv.at[1], ref.far_send, far_recv.at[1], ref.keep)
-    red.begin(lambda chip: mm(qg[tile(chip), :], w_qkv, NT))
     gb.finish()
     obuf[...] = mm(mix[...].reshape(S, hw), whole(bg), TN).astype(bf16)
     ro = ZReduce(

time: 154 us -> 149 us (0.968)
  Pallas kernels: 151 us -> 147 us
    pallas_call x1, Pallas kernels: 148 us -> 143 us  [shards(): pl.pallas_call(functools.partial(layer_kernel, names, chips, Z, sizes, al...]
where the time goes in v3:
time: 149 us
  Pallas kernels  147 us (99%)
    pallas_call x1, Pallas kernels, shards(): pl.pallas_call(functools.partial(layer_kernel, names, chips, Z, sizes, al...  143 us
    pallas_call x1, Pallas kernels, shards(): pl.pallas_call(functools.partial(hand_over, big), out_shape=[jax.ShapeDty...  3.68 us

profile of v3, /device:TPU:0, one launch (start us, length us, event | category | flops | bytes accessed | tf_op | source)
XLA Modules:
  0.0 149.1 jit_solution(8311227093200631290)
XLA Ops:
  0.6 1.4 convert_add_fusion
  2.0 143.2 %layer.1 = (bf16[128,1024]{1,0:T(8,128)(2,1)}, bf16[128,1024]{1,0:T(8,128)(2,1)}, f32[32,3072]{1,0:T(8,128)}, f32[32,1024]{1,0:T(8,128)}, f32[32,4096]{1,0:T(8,1...) custom-call(bf16[128,1024]{1,0:T(8,128)(2,1)} %bitcast.13, ...), custom_call_target="tpu_custom_call" | custom-call | tf_op jit(solution)/shard_map/layer/pallas_call | solution.py:965
  145.2 3.7 %hand_over.1 = (bf16[128,1024]{1,0:T(8,128)(2,1)}, bf16[128,1024]{1,0:T(8,128)(2,1)}, f32[32,3072]{1,0:T(8,128)}, f32[32,1024]{1,0:T(8,128)}, f32[32,4096]{1,0:T...) custom-call(bf16[128,1024]{1,0:T(8,128)(2,1)} %get-tuple-element.37., ...), custom_call_target="tpu_custom_call" | custom-call | tf_op jit(solution)/shard_map/hand_over/pallas_call | solution.py:979

commit v4 on v3

--- a/solution.py
+++ b/solution.py
@@ -408,7 +408,6 @@
         copy.start()
         return copy
 
-    load_vec = [bring(ref.vec_in, ref.vec.at[z], 0)]
     load_x = bring(x_in, xs.at[c], 1)
     if aligned:
         load_q = [
@@ -436,8 +435,11 @@
     zv, zq = ZGather(net, ref.vec), ZGather(net, ref.wqkv)
     zo, zu = ZGather(net, ref.wout_parts), ZGather(net, ref.wup)
     zd = ZGather(net, ref.wdown)
+    at = 0
+    for own, size in zip(refs[: len(sizes)], sizes):
+        ref.vec[z, :, at : at + size] = own[...].astype(f32).reshape(1, size)
+        at += size
     net.barrier()
-    load_vec[0].wait()
     zv.begin()
 
     def tokens(src, dst):
@@ -867,11 +869,6 @@
     )
     sizes = tuple(v.shape[0] for v in all_vectors)
     V, W = sum(sizes), 2 * hw + fw
-    vec_in, at = jnp.zeros((V,), f32), 0
-    for v in all_vectors:
-        vec_in = vec_in + jnp.pad(v.astype(f32), (at, V - at - v.shape[0]))
-        at += v.shape[0]
-    vec_in = vec_in[None]
     aligned = hw % 128 == 0 and fzc % 128 == 0
     wqkv_in, wup_in = qkv_weight, up_weight
     if not aligned:
@@ -890,11 +887,12 @@
         )
 
     vmem, hbm = pltpu.VMEM, pl.BlockSpec(memory_space=pl.ANY)
-    ins = dict(
+    on_chip = pl.BlockSpec(memory_space=vmem)
+    ins = {str(i): (v, on_chip) for i, v in enumerate(all_vectors)}
+    ins.update(
         x_in=(tokens_in[0], hbm),
         cot_in=(out_cotangent[0], hbm),
         docs=(doc_lengths, pl.BlockSpec(memory_space=pltpu.SMEM)),
-        vec_in=(vec_in, hbm),
         wqkv_in=(wqkv_in, hbm),
         wout_in=(out_weight, hbm),
         wup_in=(wup_in, hbm),

time: 149 us -> 148 us (level)
  no operation moved by 1% of the time
where the time goes in v4:
time: 148 us
  Pallas kernels  147 us (99%)
    pallas_call x1, Pallas kernels, shards(): pl.pallas_call(functools.partial(layer_kernel, names, chips, Z, sizes, al...  143 us
    pallas_call x1, Pallas kernels, shards(): pl.pallas_call(functools.partial(hand_over, big), out_shape=[jax.ShapeDty...  3.68 us

profile of v4, /device:TPU:0, one launch (start us, length us, event | category | flops | bytes accessed | tf_op | source)
XLA Modules:
  0.0 147.9 jit_solution(15574762796534438514)
XLA Ops:
  0.7 143.3 %layer.1 = (bf16[128,1024]{1,0:T(8,128)(2,1)}, bf16[128,1024]{1,0:T(8,128)(2,1)}, f32[32,3072]{1,0:T(8,128)}, f32[32,1024]{1,0:T(8,128)}, f32[32,4096]{1,0:T(8,1...) custom-call(bf16[256]{0:T(256)(128)(2,1)} %refs_0_.1, ...), custom_call_target="tpu_custom_call" | custom-call | tf_op jit(solution)/shard_map/layer/pallas_call | solution.py:963
  144.0 3.7 %hand_over.1 = (bf16[128,1024]{1,0:T(8,128)(2,1)}, bf16[128,1024]{1,0:T(8,128)(2,1)}, f32[32,3072]{1,0:T(8,128)}, f32[32,1024]{1,0:T(8,128)}, f32[32,4096]{1,0:T...) custom-call(bf16[128,1024]{1,0:T(8,128)(2,1)} %get-tuple-element.37., ...), custom_call_target="tpu_custom_call" | custom-call | tf_op jit(solution)/shard_map/hand_over/pallas_call | solution.py:977
